TPU v7x, 32 devices: a whole 2x2x4 slice. The times are simulated.
32 devices in a mesh: wide: 16 (over z, y, core), narrow: 2 (over x).
Axes of the slice: x: 2, y: 2, z: 4, core: 2. Of those that a mesh axis runs over, the one named last changes fastest.
Arguments:
- fields: bfloat16 [32, 48, 4, 128], P(('wide', 'narrow')), may hold values from -6 to 6
- var_ids: int32 [32, 48], P(('wide', 'narrow')), may hold values from 0 to 47, each once within a row
- slot_mask: int32 [32, 48], P(('wide', 'narrow')), may hold values from 0 to 1, as said below
- embed_table: bfloat16 [245760], P(('wide', 'narrow')), may hold values from -3 to 3
- agg_in: bfloat16 [3145728], P(('wide', 'narrow')), may hold values from -0.1875 to 0.1875
- agg_out: bfloat16 [1048576], P(('wide', 'narrow')), may hold values from -0.75 to 0.75
- attn_in: bfloat16 [3145728], P(('wide', 'narrow')), may hold values from -0.1875 to 0.1875
- attn_out: bfloat16 [1048576], P(('wide', 'narrow')), may hold values from -1.5 to 1.5
- mlp_in: bfloat16 [4194304], P(('wide', 'narrow')), may hold values from -0.1875 to 0.1875
- mlp_out: bfloat16 [4194304], P(('wide', 'narrow')), may hold values from -0.125 to 0.125
- vectors: bfloat16 [12288], P(('wide', 'narrow')), may hold values from -4 to 4, as said below
- positions: bfloat16 [131072], P(('wide', 'narrow')), may hold values from -3 to 3
- cotangent: bfloat16 [32, 128, 1024], P(('wide', 'narrow')), may hold values from -6 to 6
Outputs:
- result: bfloat16 [32, 128, 1024], P(('wide', 'narrow'))
- fields_grad: bfloat16 [32, 48, 4, 128], P(('wide', 'narrow'))
- grad_embed_table: float32 [245760], P(('wide', 'narrow'))
- grad_agg_in: float32 [3145728], P(('wide', 'narrow'))
- grad_agg_out: float32 [1048576], P(('wide', 'narrow'))
- grad_attn_in: float32 [3145728], P(('wide', 'narrow'))
- grad_attn_out: float32 [1048576], P(('wide', 'narrow'))
- grad_mlp_in: float32 [4194304], P(('wide', 'narrow'))
- grad_mlp_out: float32 [4194304], P(('wide', 'narrow'))
- grad_vectors: float32 [12288], P(('wide', 'narrow'))
- grad_positions: float32 [131072], P(('wide', 'narrow'))
Inputs may be any that keep to these rules, and one draw needn't show every extreme that they name: `slot_mask`: each sample has 8 to 48 live slots; some sample has exactly 48 and some exactly 8. `var_ids`: each sample's slots name every variable once. `vectors`: rows 1 and 5 lie within 0.6 to 1.4.
All inputs are finite; a program needn't handle non-finite values.
Results may differ from a plain program's by a relative error of at most 0.029.
Values may be sent and summed in bfloat16 or wider, within the bound.
A program may use at most 320 MiB of HBM per device.

v0:
```python
import jax
import jax.numpy as jnp
from jax import lax
from jax.sharding import PartitionSpec as P

D = 1024
HEADS = 16
FF = 4096
VARS = 48
PATCH_PIXELS = 4
PATCHES = 128
VEC_ROWS = 12


norm_eps = 1e-05
masked_score = -1e30
highest_precision = lax.Precision.HIGHEST


def layer_norm(values, gain_row, shift_row):
    centre = jnp.mean(values, -1, keepdims=True)
    centred = values - centre
    spread = jnp.mean(centred * centred, -1, keepdims=True)
    return centred * lax.rsqrt(spread + norm_eps) * gain_row + shift_row


def gelu_exact(values):
    return 0.5 * values * (1.0 + lax.erf(values * 0.7071067811865476))


def softmax_rows(scores):
    highest_score = jnp.max(scores, -1, keepdims=True)
    expo = jnp.exp(scores - highest_score)
    return expo / jnp.sum(expo, -1, keepdims=True)


def unpack(gathered):
    return (
        gathered[0].reshape(VARS, (PATCH_PIXELS + 1) * D),
        gathered[1].reshape(D, 3 * D),
        gathered[2].reshape(D, D),
        gathered[3].reshape(D, 3 * D),
        gathered[4].reshape(D, D),
        gathered[5].reshape(D, FF),
        gathered[6].reshape(FF, D),
        gathered[7].reshape(VEC_ROWS, D),
        gathered[8].reshape(PATCHES, D),
    )


def on_device(
    fields,
    var_ids,
    slot_mask,
    embed_table,
    agg_in,
    agg_out,
    attn_in,
    attn_out,
    mlp_in,
    mlp_out,
    vectors,
    positions,
    cotangent,
):
    gathered = (
        lax.all_gather(embed_table, ("wide", "narrow"), axis=0, tiled=True),
        lax.all_gather(agg_in, ("wide", "narrow"), axis=0, tiled=True),
        lax.all_gather(agg_out, ("wide", "narrow"), axis=0, tiled=True),
        lax.all_gather(attn_in, ("wide", "narrow"), axis=0, tiled=True),
        lax.all_gather(attn_out, ("wide", "narrow"), axis=0, tiled=True),
        lax.all_gather(mlp_in, ("wide", "narrow"), axis=0, tiled=True),
        lax.all_gather(mlp_out, ("wide", "narrow"), axis=0, tiled=True),
        lax.all_gather(vectors, ("wide", "narrow"), axis=0, tiled=True),
        lax.all_gather(positions, ("wide", "narrow"), axis=0, tiled=True),
    )
    (
        table_full,
        agg_in_full,
        agg_out_full,
        attn_in_full,
        attn_out_full,
        mlp_in_full,
        mlp_out_full,
        vector_rows,
        position_rows,
    ) = unpack(gathered)
    head_size = D // HEADS
    score_scale = head_size ** (-0.5)
    length = PATCHES
    single_float = jnp.float32
    bf16 = jnp.bfloat16
    pixel_values = fields[0]
    onehot = (var_ids[0][:, None] == jnp.arange(VARS)[None, :]).astype(bf16)
    slot_lookup_table = jnp.dot(onehot, table_full, preferred_element_type=single_float).reshape(
        VARS, PATCH_PIXELS + 1, D
    )
    patch_row_block = slot_lookup_table[:, :PATCH_PIXELS].astype(bf16)
    token_rows = (
        jnp.einsum(
            "tnz,tnu->tzu", pixel_values, patch_row_block, preferred_element_type=single_float
        )
        + slot_lookup_table[:, PATCH_PIXELS][:, None, :]
    )
    token_rows = token_rows.astype(bf16)
    query_row = vector_rows[0]
    agg_query = jnp.dot(
        query_row[None, :], agg_in_full[:, :D], preferred_element_type=single_float
    )[0].astype(bf16)
    flat_tokens = token_rows.reshape(VARS * length, D)
    key_value = jnp.dot(
        flat_tokens, agg_in_full[:, D:], preferred_element_type=single_float
    ).astype(bf16)
    slot_keys = key_value[:, :D].reshape(VARS, length, HEADS, head_size)
    slot_values = key_value[:, D:].reshape(VARS, length, HEADS, head_size)
    live_slots = slot_mask[0] > 0
    agg_scores = (
        jnp.einsum(
            "hc,slhc->lhs",
            agg_query.reshape(HEADS, head_size),
            slot_keys,
            preferred_element_type=single_float,
        )
        * score_scale
    )
    agg_scores = jnp.where(live_slots[None, None, :], agg_scores, masked_score)
    agg_probs = softmax_rows(agg_scores)
    agg_probs_low = agg_probs.astype(bf16)
    mixture = (
        jnp.einsum("lhs,slhc->lhc", agg_probs_low, slot_values, preferred_element_type=single_float)
        .reshape(length, D)
        .astype(bf16)
    )
    row_values = vector_rows.astype(single_float)
    position_values = position_rows.astype(single_float)
    stream = jnp.dot(mixture, agg_out_full, preferred_element_type=single_float) + position_values
    normed1 = layer_norm(stream, row_values[1], row_values[2]).astype(bf16)
    qkv_bias = jnp.concatenate([row_values[3], jnp.zeros((2 * D,), single_float)])
    projected = (
        jnp.dot(normed1, attn_in_full, preferred_element_type=single_float) + qkv_bias
    ).astype(bf16)
    queries = projected[:, :D].reshape(length, HEADS, head_size)
    keys = projected[:, D : 2 * D].reshape(length, HEADS, head_size)
    values = projected[:, 2 * D :].reshape(length, HEADS, head_size)
    self_scores = (
        jnp.einsum("ihc,jhc->hij", queries, keys, preferred_element_type=single_float) * score_scale
    )
    score_peak = jnp.max(self_scores, -1, keepdims=True)
    self_lse = score_peak + jnp.log(jnp.sum(jnp.exp(self_scores - score_peak), -1, keepdims=True))
    probs_low = jnp.exp(self_scores - self_lse).astype(bf16)
    attended = (
        jnp.einsum("hij,jhc->ihc", probs_low, values, preferred_element_type=single_float)
        .reshape(length, D)
        .astype(bf16)
    )
    stream1 = (
        stream
        + jnp.dot(attended, attn_out_full, preferred_element_type=single_float)
        + row_values[4]
    )
    normed2 = layer_norm(stream1, row_values[5], row_values[6]).astype(bf16)
    hidden = jnp.dot(normed2, mlp_in_full, preferred_element_type=single_float) + row_values[
        8:VEC_ROWS
    ].reshape(FF)
    activated = gelu_exact(hidden).astype(bf16)
    result = (
        stream1
        + jnp.dot(activated, mlp_out_full, preferred_element_type=single_float)
        + row_values[7]
    ).astype(bf16)
    regathered = (
        lax.all_gather(embed_table, ("wide", "narrow"), axis=0, tiled=True),
        lax.all_gather(agg_in, ("wide", "narrow"), axis=0, tiled=True),
        lax.all_gather(agg_out, ("wide", "narrow"), axis=0, tiled=True),
        lax.all_gather(attn_in, ("wide", "narrow"), axis=0, tiled=True),
        lax.all_gather(attn_out, ("wide", "narrow"), axis=0, tiled=True),
        lax.all_gather(mlp_in, ("wide", "narrow"), axis=0, tiled=True),
        lax.all_gather(mlp_out, ("wide", "narrow"), axis=0, tiled=True),
        lax.all_gather(vectors, ("wide", "narrow"), axis=0, tiled=True),
        lax.all_gather(positions, ("wide", "narrow"), axis=0, tiled=True),
    )
    (
        table_full,
        agg_in_full,
        agg_out_full,
        attn_in_full,
        attn_out_full,
        mlp_in_full,
        mlp_out_full,
        vector_rows,
        position_rows,
    ) = unpack(regathered)
    grad_output = cotangent[0].astype(single_float)
    grad_branch2 = grad_output.astype(bf16)
    grad_fc2_bias = jnp.sum(grad_branch2.astype(single_float), 0)
    grad_mlp_out = jnp.dot(activated.T, grad_branch2, preferred_element_type=single_float)
    grad_activated = jnp.dot(grad_branch2, mlp_out_full.T, preferred_element_type=single_float)
    gelu_value, gelu_pull = jax.vjp(gelu_exact, hidden)
    grad_hidden = gelu_pull(grad_activated)[0].astype(bf16)
    grad_fc1_bias = jnp.sum(grad_hidden.astype(single_float), 0)
    grad_mlp_in = jnp.dot(normed2.T, grad_hidden, preferred_element_type=single_float)
    grad_normed2 = jnp.dot(grad_hidden, mlp_in_full.T, preferred_element_type=single_float)
    norm_value2, norm2_pull = jax.vjp(layer_norm, stream1, row_values[5], row_values[6])
    back_stream1, grad_gain2, grad_shift2 = norm2_pull(grad_normed2)
    grad_stream1 = grad_output + back_stream1
    grad_branch1 = grad_stream1.astype(bf16)
    grad_proj_bias = jnp.sum(grad_branch1.astype(single_float), 0)
    grad_attn_out = jnp.dot(attended.T, grad_branch1, preferred_element_type=single_float)
    grad_attended = (
        jnp.dot(grad_branch1, attn_out_full.T, preferred_element_type=single_float)
        .astype(bf16)
        .reshape(length, HEADS, head_size)
    )
    again_scores = (
        jnp.einsum("ihc,jhc->hij", queries, keys, preferred_element_type=single_float) * score_scale
    )
    again_probs = jnp.exp(again_scores - self_lse)
    again_low = again_probs.astype(bf16)
    grad_probs = jnp.einsum(
        "ihc,jhc->hij", grad_attended, values, preferred_element_type=single_float
    )
    grad_self_scores = (
        again_probs * (grad_probs - jnp.sum(again_probs * grad_probs, -1, keepdims=True))
    ).astype(bf16)
    grad_queries = (
        jnp.einsum("hij,jhc->ihc", grad_self_scores, keys, preferred_element_type=single_float)
        * score_scale
    )
    grad_keys = (
        jnp.einsum("hij,ihc->jhc", grad_self_scores, queries, preferred_element_type=single_float)
        * score_scale
    )
    grad_values = jnp.einsum(
        "hij,ihc->jhc", again_low, grad_attended, preferred_element_type=single_float
    )
    grad_projected = jnp.concatenate(
        [
            grad_queries.reshape(length, D),
            grad_keys.reshape(length, D),
            grad_values.reshape(length, D),
        ],
        1,
    ).astype(bf16)
    grad_query_bias = jnp.sum(grad_projected[:, :D].astype(single_float), 0)
    grad_attn_in = jnp.dot(normed1.T, grad_projected, preferred_element_type=single_float)
    grad_normed1 = jnp.dot(grad_projected, attn_in_full.T, preferred_element_type=single_float)
    norm_value1, norm1_pull = jax.vjp(layer_norm, stream, row_values[1], row_values[2])
    back_stream, grad_gain1, grad_shift1 = norm1_pull(grad_normed1)
    grad_stream = grad_stream1 + back_stream
    grad_agg_branch = grad_stream.astype(bf16)
    grad_agg_out = jnp.dot(mixture.T, grad_agg_branch, preferred_element_type=single_float)
    grad_mixture = (
        jnp.dot(grad_agg_branch, agg_out_full.T, preferred_element_type=single_float)
        .astype(bf16)
        .reshape(length, HEADS, head_size)
    )
    grad_agg_probs = jnp.einsum(
        "lhc,slhc->lhs", grad_mixture, slot_values, preferred_element_type=single_float
    )
    grad_agg_scores = (
        agg_probs * (grad_agg_probs - jnp.sum(agg_probs * grad_agg_probs, -1, keepdims=True))
    ).astype(bf16)
    grad_slot_values = jnp.einsum(
        "lhs,lhc->slhc", agg_probs_low, grad_mixture, preferred_element_type=single_float
    )
    grad_slot_keys = (
        jnp.einsum(
            "lhs,hc->slhc",
            grad_agg_scores,
            agg_query.reshape(HEADS, head_size),
            preferred_element_type=single_float,
        )
        * score_scale
    )
    grad_agg_query = (
        jnp.einsum("lhs,slhc->hc", grad_agg_scores, slot_keys, preferred_element_type=single_float)
        * score_scale
    ).reshape(D)
    grad_key_value = jnp.concatenate(
        [grad_slot_keys.reshape(VARS * length, D), grad_slot_values.reshape(VARS * length, D)], 1
    ).astype(bf16)
    grad_agg_kv = jnp.dot(flat_tokens.T, grad_key_value, preferred_element_type=single_float)
    grad_token_rows = (
        jnp.dot(grad_key_value, agg_in_full[:, D:].T, preferred_element_type=single_float)
        .astype(bf16)
        .reshape(VARS, length, D)
    )
    grad_agg_qproj = query_row.astype(single_float)[:, None] * grad_agg_query[None, :]
    grad_query_row = jnp.dot(
        agg_in_full[:, :D].astype(single_float), grad_agg_query, precision=highest_precision
    )
    grad_agg_in = jnp.concatenate([grad_agg_qproj, grad_agg_kv], 1)
    grad_patch_rows = jnp.einsum(
        "hzo,how->hzw", pixel_values, grad_token_rows, preferred_element_type=single_float
    )
    grad_embed = jnp.sum(grad_token_rows.astype(single_float), 1)
    grad_slots = jnp.concatenate([grad_patch_rows, grad_embed[:, None, :]], 1).reshape(
        VARS, (PATCH_PIXELS + 1) * D
    )
    grad_table = jnp.dot(onehot.astype(single_float).T, grad_slots, precision=highest_precision)
    fields_grad = jnp.einsum(
        "cyi,cgi->cgy", grad_token_rows, patch_row_block, preferred_element_type=single_float
    ).astype(bf16)
    grad_rows = jnp.concatenate(
        [
            jnp.stack(
                [
                    grad_query_row,
                    grad_gain1,
                    grad_shift1,
                    grad_query_bias,
                    grad_proj_bias,
                    grad_gain2,
                    grad_shift2,
                    grad_fc2_bias,
                ]
            ),
            grad_fc1_bias.reshape(FF // D, D),
        ],
        0,
    )
    wide_count = lax.axis_size("wide")
    narrow_count = lax.axis_size("narrow")
    block_table = grad_table.reshape(wide_count, narrow_count, -1)
    block_agg_in = grad_agg_in.reshape(wide_count, narrow_count, -1)
    block_agg_out = grad_agg_out.reshape(wide_count, narrow_count, -1)
    block_attn_in = grad_attn_in.reshape(wide_count, narrow_count, -1)
    block_attn_out = grad_attn_out.reshape(wide_count, narrow_count, -1)
    block_mlp_in = grad_mlp_in.reshape(wide_count, narrow_count, -1)
    block_mlp_out = grad_mlp_out.reshape(wide_count, narrow_count, -1)
    block_rows = grad_rows.reshape(wide_count, narrow_count, -1)
    block_positions = grad_stream.reshape(wide_count, narrow_count, -1)
    regrouped = (
        lax.all_to_all(
            block_table.astype(jnp.bfloat16), "narrow", split_axis=1, concat_axis=1, tiled=True
        ).astype(block_table.dtype),
        lax.all_to_all(
            block_agg_in.astype(jnp.bfloat16), "narrow", split_axis=1, concat_axis=1, tiled=True
        ).astype(block_agg_in.dtype),
        lax.all_to_all(
            block_agg_out.astype(jnp.bfloat16), "narrow", split_axis=1, concat_axis=1, tiled=True
        ).astype(block_agg_out.dtype),
        lax.all_to_all(
            block_attn_in.astype(jnp.bfloat16), "narrow", split_axis=1, concat_axis=1, tiled=True
        ).astype(block_attn_in.dtype),
        lax.all_to_all(
            block_attn_out.astype(jnp.bfloat16), "narrow", split_axis=1, concat_axis=1, tiled=True
        ).astype(block_attn_out.dtype),
        lax.all_to_all(
            block_mlp_in.astype(jnp.bfloat16), "narrow", split_axis=1, concat_axis=1, tiled=True
        ).astype(block_mlp_in.dtype),
        lax.all_to_all(
            block_mlp_out.astype(jnp.bfloat16), "narrow", split_axis=1, concat_axis=1, tiled=True
        ).astype(block_mlp_out.dtype),
        lax.all_to_all(
            block_rows.astype(jnp.bfloat16), "narrow", split_axis=1, concat_axis=1, tiled=True
        ).astype(block_rows.dtype),
        lax.all_to_all(
            block_positions.astype(jnp.bfloat16), "narrow", split_axis=1, concat_axis=1, tiled=True
        ).astype(block_positions.dtype),
    )
    partial_sums = tuple((jnp.sum(member, 1) for member in regrouped))
    summed = (
        lax.psum_scatter(
            partial_sums[0].astype(jnp.bfloat16), "wide", scatter_dimension=0, tiled=True
        ).astype(jnp.float32),
        lax.psum_scatter(
            partial_sums[1].astype(jnp.bfloat16), "wide", scatter_dimension=0, tiled=True
        ).astype(jnp.float32),
        lax.psum_scatter(
            partial_sums[2].astype(jnp.bfloat16), "wide", scatter_dimension=0, tiled=True
        ).astype(jnp.float32),
        lax.psum_scatter(
            partial_sums[3].astype(jnp.bfloat16), "wide", scatter_dimension=0, tiled=True
        ).astype(jnp.float32),
        lax.psum_scatter(
            partial_sums[4].astype(jnp.bfloat16), "wide", scatter_dimension=0, tiled=True
        ).astype(jnp.float32),
        lax.psum_scatter(
            partial_sums[5].astype(jnp.bfloat16), "wide", scatter_dimension=0, tiled=True
        ).astype(jnp.float32),
        lax.psum_scatter(
            partial_sums[6].astype(jnp.bfloat16), "wide", scatter_dimension=0, tiled=True
        ).astype(jnp.float32),
        lax.psum_scatter(
            partial_sums[7].astype(jnp.bfloat16), "wide", scatter_dimension=0, tiled=True
        ).astype(jnp.float32),
        lax.psum_scatter(
            partial_sums[8].astype(jnp.bfloat16), "wide", scatter_dimension=0, tiled=True
        ).astype(jnp.float32),
    )
    return (
        result[None],
        fields_grad[None],
        summed[0].reshape(-1),
        summed[1].reshape(-1),
        summed[2].reshape(-1),
        summed[3].reshape(-1),
        summed[4].reshape(-1),
        summed[5].reshape(-1),
        summed[6].reshape(-1),
        summed[7].reshape(-1),
        summed[8].reshape(-1),
    )


def solution(mesh):
    return jax.shard_map(
        on_device,
        mesh=mesh,
        in_specs=(
            P(("wide", "narrow"), None, None, None),
            P(("wide", "narrow"), None),
            P(("wide", "narrow"), None),
            P(("wide", "narrow")),
            P(("wide", "narrow")),
            P(("wide", "narrow")),
            P(("wide", "narrow")),
            P(("wide", "narrow")),
            P(("wide", "narrow")),
            P(("wide", "narrow")),
            P(("wide", "narrow")),
            P(("wide", "narrow")),
            P(("wide", "narrow"), None, None),
        ),
        out_specs=(
            P(("wide", "narrow"), None, None),
            P(("wide", "narrow"), None, None, None),
            P(("wide", "narrow")),
            P(("wide", "narrow")),
            P(("wide", "narrow")),
            P(("wide", "narrow")),
            P(("wide", "narrow")),
            P(("wide", "narrow")),
            P(("wide", "narrow")),
            P(("wide", "narrow")),
            P(("wide", "narrow")),
        ),
        check_vma=False,
    )
```

profile of v0, /device:TPU:8, one launch (start us, length us, event | category | flops | bytes accessed | tf_op | source)
XLA Modules:
  0.0 1346.0 jit_solution(5315944718794112123)
XLA Ops:
  12.6 56.4 %all-gather.1 = bf16[32,1,384]{2,1,0:T(2,128)(2,1)S(1)} all-gather(bf16[1,1,384]{2,1,0:T(2,128)(2,1)S(1)} %reshape.378), channel_id=1, replica_groups=mesh['wide'=16,'narrow'=2] {'wide','narrow'}, dimensions={0}, use_global_device_ids=true | all-gather | bytes 25344 | tf_op jit(solution)/shard_map/all_gather | solution.py:74
  69.8 64.8 %all_gather.37 = bf16[131072]{0:T(1024)(128)(2,1)S(1)} all-gather(bf16[4096]{0:T(1024)(128)(2,1)} %param.24), channel_id=1, replica_groups=mesh['wide'=16,'narrow'=2] {'wide','narrow'}, dimensions={0}, use_global_device_ids=true | all-gather | bytes 270336 | tf_op jit(solution)/shard_map/all_gather | solution.py:75
  134.7 73.9 %all-gather = bf16[32,1,7680]{2,1,0:T(2,128)(2,1)S(1)} all-gather(bf16[1,1,7680]{2,1,0:T(2,128)(2,1)S(1)} %reshape.376), channel_id=1, replica_groups=mesh['wide'=16,'narrow'=2] {'wide','narrow'}, dimensions={0}, use_global_device_ids=true | all-gather | bytes 506880 | tf_op jit(solution)/shard_map/all_gather | solution.py:67
  228.0 10.3 reshape.312
  241.0 33.4 %convolution_convert_fusion = bf16[6144,2048]{1,0:T(8,128)(2,1)} fusion(bf16[6144,1024]{1,0:T(8,128)(2,1)} %bitcast.165, bf16[1024,3072]{1,0:T(8,128)(2,1)} %reshape.312), kind=kOutput, calls=%fused_computation.9 | convolution fusion | flops 25782386688 | bytes 41943040 | tf_op jit(solution)/shard_map/dot_general | solution.py:111
  274.4 17.5 %fusion.71 = (bf16[6144,1024]{1,0:T(8,128)(2,1)}, bf16[6144,1024]{1,0:T(8,128)(2,1)}) fusion(bf16[6144,2048]{1,0:T(8,128)(2,1)} %convolution_convert_fusion), kind=kLoop, calls=%fused_computation.146 | loop fusion | bytes 50331648 | tf_op jit(solution)/shard_map/slice | solution.py:115
  291.9 16.5 %copy.79 = bf16[6144,1024]{0,1:T(8,128)(2,1)} copy(bf16[6144,1024]{1,0:T(8,128)(2,1)} %get-tuple-element.31) | data formatting | bytes 25165824 | tf_op jit(solution)/shard_map/slice | solution.py:115
  308.4 11.8 copy.125
  320.2 32.8 %reshape.394 = bf16[48,128,16,64]{3,2,1,0:T(8,128)(2,1)} reshape(bf16[6144,1024]{1,0:T(8,128)(2,1)} %get-tuple-element.32) | data formatting | bytes 25165824 | tf_op jit(solution)/shard_map/reshape | solution.py:114
  353.0 27.1 %copy.99 = bf16[48,128,16,64]{1,3,0,2:T(8,128)(2,1)} copy(bf16[48,128,16,64]{3,2,1,0:T(8,128)(2,1)} %reshape.394) | data formatting | bytes 25165824 | tf_op jit(solution)/shard_map/reshape | solution.py:114
  380.1 10.3 reshape.316
  399.5 10.3 multiply_reduce_fusion.1
  419.3 13.5 reshape.321
  437.7 14.1 %reshape.322 = bf16[4096,1024]{1,0:T(8,128)(2,1)} reshape(bf16[4194304]{0:T(1024)(128)(2,1)} %all-gather.19.cloned.1.call-done) | data formatting | bytes 16777216 | tf_op jit(solution)/shard_map/reshape | solution.py:45
  477.1 12.5 multiply_convert_fusion
  497.3 15.0 %bitcast_dynamic-update-slice_fusion.1 = bf16[6144,2048]{0,1:T(8,128)(2,1)} fusion(bf16[128,8,48,128]{3,2,1,0:T(8,128)(2,1)} %bitcast.161), kind=kLoop, calls=%fused_computation.11 | loop fusion | bytes 25165824
  512.3 14.8 %bitcast_dynamic-update-slice_fusion = bf16[6144,2048]{0,1:T(8,128)(2,1)} fusion(bf16[6144,2048]{0,1:T(8,128)(2,1)} %bitcast_dynamic-update-slice_fusion.1, bf16[128,8,48,128]{3,2,1,0:T(8,128)(2,1)S(1)} %bitcast.160), kind=kLoop, calls=%fused_computation.10 | loop fusion | bytes 25165824 | tf_op jit(solution)/shard_map/concatenate | solution.py:279
  527.1 32.1 %convolution_convert_fusion.1 = bf16[6144,1024]{1,0:T(8,128)(2,1)} fusion(bf16[6144,2048]{0,1:T(8,128)(2,1)} %bitcast_dynamic-update-slice_fusion, bf16[1024,3072]{1,0:T(8,128)(2,1)S(1)} %bitcast.164), kind=kOutput, calls=%fused_computation.12 | convolution fusion | flops 25776095232 | bytes 41943040 | tf_op jit(solution)/shard_map/dot_general | solution.py:284
  608.1 14.0 %all-to-all-done.2 = bf16[16,2,32768]{2,0,1:T(8,128)(2,1)} async-done(((bf16[16,2,32768]{2,0,1:T(8,128)(2,1)}), bf16[16,2,32768]{2,0,1:T(8,128)(2,1)}, u32[]{:S(2)}, u32[]{:S(2)}) %all-to-all-start.2) | async-done | bytes 2097184 | tf_op jit(solution)/shard_map/all_to_all | solution.py:340
  631.4 12.9 convert_element_type.234
  660.8 34.5 %convolution_convert_fusion.6 = bf16[1024,2048]{1,0:T(8,128)(2,1)} fusion(bf16[6144,1024]{1,0:T(8,128)(2,1)} %bitcast.166, bf16[6144,2048]{0,1:T(8,128)(2,1)} %bitcast_dynamic-update-slice_fusion), kind=kOutput, calls=%fused_computation.20 | convolution fusion | flops 25771900928 | bytes 41943040 | tf_op jit(solution)/shard_map/dot_general | solution.py:282
  707.3 13.1 convert_element_type.230
  720.5 8.9 copy.91
  740.4 14.5 %convert_element_type.240 = bf16[16,2,131072]{2,1,0:T(2,128)(2,1)} reshape(bf16[4096,1024]{1,0:T(8,128)(2,1)} %convolution_convert_fusion.2) | data formatting | bytes 16777216 | tf_op jit(solution)/shard_map/convert_element_type | solution.py:353
  754.9 11.2 copy.96
  766.1 35.8 %all-to-all-done.1 = bf16[16,2,98304]{2,0,1:T(8,128)(2,1)} async-done(((bf16[16,2,98304]{2,0,1:T(8,128)(2,1)}), bf16[16,2,98304]{2,0,1:T(8,128)(2,1)}, u32[]{:S(2)}, u32[]{:S(2)}) %all-to-all-start.1) | async-done | bytes 6291488 | tf_op jit(solution)/shard_map/all_to_all | solution.py:337
  816.2 14.5 %convert_element_type.238 = bf16[16,2,131072]{2,1,0:T(2,128)(2,1)} reshape(bf16[1024,4096]{1,0:T(8,128)(2,1)} %convolution_convert_fusion.3) | data formatting | bytes 16777216 | tf_op jit(solution)/shard_map/convert_element_type | solution.py:350
  830.6 11.2 copy.95
  841.8 55.0 %all-to-all-done.6 = bf16[16,2,131072]{2,0,1:T(8,128)(2,1)} async-done(((bf16[16,2,131072]{2,0,1:T(8,128)(2,1)}), bf16[16,2,131072]{2,0,1:T(8,128)(2,1)}, u32[]{:S(2)}, u32[]{:S(2)}) %all-to-all-start.6) | async-done | bytes 8388640 | tf_op jit(solution)/shard_map/all_to_all | solution.py:352
  933.7 56.9 %all-to-all-done.5 = bf16[16,2,131072]{2,0,1:T(8,128)(2,1)} async-done(((bf16[16,2,131072]{2,0,1:T(8,128)(2,1)}), bf16[16,2,131072]{2,0,1:T(8,128)(2,1)}, u32[]{:S(2)}, u32[]{:S(2)}) %all-to-all-start.5) | async-done | bytes 8388640 | tf_op jit(solution)/shard_map/all_to_all | solution.py:349
  1020.0 76.5 %all-reduce.8 = bf16[16,384]{1,0:T(8,128)(2,1)S(1)} all-reduce(bf16[16,384]{1,0:T(8,128)(2,1)S(1)} %reduce_sum.373), channel_id=9, replica_groups=mesh['wide'=16,'narrow'=2] {'wide'}, use_global_device_ids=true, to_apply=%region_38.39.clone | all-reduce | flops 6144 | bytes 24576
  1097.8 225.2 %all-reduce.13.cloned.1.call-done = (bf16[16,7680]{1,0:T(8,128)(2,1)}, bf16[16,98304]{1,0:T(8,128)(2,1)}, bf16[16,32768]{1,0:T(8,128)(2,1)}, bf16[16,98304]{1,0:...) async-done(((bf16[16,7680]{1,0:T(8,128)(2,1)}, bf16[16,98304]{1,0:T(8,128)(2,1)}, ...) | async-done | bytes 17154064
  (297 shorter events, 279.4 us)
Async XLA Ops:
  7.2 206.5 %copy-start = (bf16[1,48,4,128]{3,2,1,0:T(4,128)(2,1)S(1)}, bf16[1,48,4,128]{3,2,1,0:T(4,128)(2,1)}, u32[]{:S(2)}) copy-start(bf16[1,48,4,128]{3,2,1,0:T(4,128)(2,1)} %param.13) | copy-start | bytes 147460
  7.2 206.4 %copy-start.60 = (s32[1,48]{1,0:T(1,128)S(1)}, s32[1,48]{1,0:T(1,128)}, u32[]{:S(2)}) copy-start(s32[1,48]{1,0:T(1,128)} %param.15) | copy-start | bytes 580
  7.2 213.3 %all-gather.11.cloned.1.call-start = ((), (), s32[]{:S(2)}) async-start(), calls=%async_computation.10 | async-start | bytes 2162688 | tf_op jit(solution)/shard_map/all_gather | solution.py:69
  7.9 215.5 %all-gather.15.cloned.1.call-start = ((), (), s32[]{:S(2)}) async-start(), calls=%async_computation.12 | async-start | bytes 2162688 | tf_op jit(solution)/shard_map/all_gather | solution.py:71
  8.7 219.3 %all-gather.9.cloned.1.call-start = ((), (), s32[]{:S(2)}) async-start(), calls=%async_computation.9 | async-start | bytes 6488064 | tf_op jit(solution)/shard_map/all_gather | solution.py:68
  9.4 370.7 %all-gather.13.cloned.1.call-start = ((), (), s32[]{:S(2)}) async-start(), calls=%async_computation.11 | async-start | bytes 6488064 | tf_op jit(solution)/shard_map/all_gather | solution.py:70
  10.0 409.3 %all-gather.17.cloned.1.call-start = ((), (), s32[]{:S(2)}) async-start(), calls=%async_computation.13 | async-start | bytes 8650752 | tf_op jit(solution)/shard_map/all_gather | solution.py:72
  10.6 427.1 %all-gather.19.cloned.1.call-start = ((), (), s32[]{:S(2)}) async-start(), calls=%async_computation.14 | async-start | bytes 8650752 | tf_op jit(solution)/shard_map/all_gather | solution.py:73
  213.6 219.2 %copy-start.43 = (f32[1024]{0:T(1024)}, f32[1024]{0:T(1024)S(1)}, u32[]{:S(2)}) copy-start(f32[1024]{0:T(1024)S(1)} %get-tuple-element.41) | copy-start | bytes 12292
  213.6 249.5 %copy-start.40 = (f32[1024]{0:T(1024)}, f32[1024]{0:T(1024)S(1)}, u32[]{:S(2)}) copy-start(f32[1024]{0:T(1024)S(1)} %get-tuple-element.40) | copy-start | bytes 12292
  223.4 186.4 %copy-start.10 = (bf16[1024,1024]{1,0:T(8,128)(2,1)}, bf16[1024,1024]{1,0:T(8,128)(2,1)S(1)}, u32[]{:S(2)}) copy-start(bf16[1024,1024]{1,0:T(8,128)(2,1)S(1)} %reshape.315) | copy-start | bytes 6291460
  418.3 44.9 %copy-start.46 = (f32[128]{0:T(128)}, f32[128]{0:T(128)S(1)}, u32[]{:S(2)}) copy-start(f32[128]{0:T(128)S(1)} %broadcast_multiply_fusion.1) | copy-start | bytes 1540
  419.3 43.9 %copy-start.48 = (f32[128]{0:T(128)}, f32[128]{0:T(128)S(1)}, u32[]{:S(2)}) copy-start(f32[128]{0:T(128)S(1)} %fusion.58) | copy-start | bytes 1540
  497.2 29.8 %slice-start.3 = ((s8[6291456]{0:T(1024)(128)(4,1)}), s8[4194304]{0:T(1024)(128)(4,1)S(1)}, s32[]{:S(2)}) async-start(s8[6291456]{0:T(1024)(128)(4,1)} %bitcast.163), calls=%async_computation.19 | async-start | bytes 8388608
  574.3 9.2 all-to-all-start.8
  583.5 11.8 all-to-all-start
  595.3 26.8 %all-to-all-start.2 = ((bf16[16,2,32768]{2,0,1:T(8,128)(2,1)}), bf16[16,2,32768]{2,0,1:T(8,128)(2,1)}, u32[]{:S(2)}, u32[]{:S(2)}) async-start(bf16[16,2,32768]{2,0,1:T(8,128)(2,1)} %copy.92), calls=%async_computation.2 | async-start | bytes 4194304 | tf_op jit(solution)/shard_map/all_to_all | solution.py:340
  600.8 25.0 %copy-start.34 = (bf16[16,64,128]{2,1,0:T(8,128)(2,1)S(1)}, bf16[16,64,128]{2,1,0:T(8,128)(2,1)}, u32[]{:S(2)}) copy-start(bf16[16,64,128]{2,1,0:T(8,128)(2,1)} %copy-done.33) | copy-start | bytes 786436
  622.1 31.0 %all-to-all-start.4 = ((bf16[16,2,32768]{2,0,1:T(8,128)(2,1)}), bf16[16,2,32768]{2,0,1:T(8,128)(2,1)S(1)}, u32[]{:S(2)}, u32[]{:S(2)}) async-start(bf16[16,2,32768]{2,0,1:T(8,128)(2,1)} %copy.94), calls=%async_computation.4 | async-start | bytes 4194304 | tf_op jit(solution)/shard_map/all_to_all | solution.py:346
  654.5 74.9 %all-to-all-start.3 = ((bf16[16,2,98304]{2,0,1:T(8,128)(2,1)}), bf16[16,2,98304]{2,0,1:T(8,128)(2,1)}, u32[]{:S(2)}, u32[]{:S(2)}) async-start(bf16[16,2,98304]{2,0,1:T(8,128)(2,1)} %copy.93), calls=%async_computation.3 | async-start | bytes 12582912 | tf_op jit(solution)/shard_map/all_to_all | solution.py:343
  660.7 34.5 %copy-start.39 = (bf16[128,16,48]{0,2,1:T(8,128)(2,1)S(1)}, bf16[128,16,48]{0,2,1:T(8,128)(2,1)}, u32[]{:S(2)}) copy-start(bf16[128,16,48]{0,2,1:T(8,128)(2,1)} %copy-done.38) | copy-start | bytes 589828
  729.3 72.5 %all-to-all-start.1 = ((bf16[16,2,98304]{2,0,1:T(8,128)(2,1)}), bf16[16,2,98304]{2,0,1:T(8,128)(2,1)}, u32[]{:S(2)}, u32[]{:S(2)}) async-start(bf16[16,2,98304]{2,0,1:T(8,128)(2,1)} %copy.91), calls=%async_computation.1 | async-start | bytes 12582912 | tf_op jit(solution)/shard_map/all_to_all | solution.py:337
  766.1 43.2 %copy-start.7 = (f32[128,1024]{1,0:T(8,128)S(1)}, f32[128,1024]{1,0:T(8,128)}, u32[]{:S(2)}) copy-start(f32[128,1024]{1,0:T(8,128)} %copy-done.5) | copy-start | bytes 1572868
  766.1 43.2 %copy-start.41 = (f32[1024]{0:T(1024)S(1)}, f32[1024]{0:T(1024)}, u32[]{:S(2)}) copy-start(f32[1024]{0:T(1024)} %copy-done.40) | copy-start | bytes 12292
  766.1 43.2 %copy-start.44 = (f32[1024]{0:T(1024)S(1)}, f32[1024]{0:T(1024)}, u32[]{:S(2)}) copy-start(f32[1024]{0:T(1024)} %copy-done.43) | copy-start | bytes 12292
  766.1 43.2 %copy-start.47 = (f32[128]{0:T(128)S(1)}, f32[128]{0:T(128)}, u32[]{:S(2)}) copy-start(f32[128]{0:T(128)} %copy-done.46) | copy-start | bytes 1540
  766.1 43.2 %copy-start.49 = (f32[128]{0:T(128)S(1)}, f32[128]{0:T(128)}, u32[]{:S(2)}) copy-start(f32[128]{0:T(128)} %copy-done.48) | copy-start | bytes 1540
  801.9 95.0 %all-to-all-start.6 = ((bf16[16,2,131072]{2,0,1:T(8,128)(2,1)}), bf16[16,2,131072]{2,0,1:T(8,128)(2,1)}, u32[]{:S(2)}, u32[]{:S(2)}) async-start(bf16[16,2,131072]{2,0,1:T(8,128)(2,1)} %copy.96), calls=%async_computation.6 | async-start | bytes 16777216 | tf_op jit(solution)/shard_map/all_to_all | solution.py:352
  896.9 93.7 %all-to-all-start.5 = ((bf16[16,2,131072]{2,0,1:T(8,128)(2,1)}), bf16[16,2,131072]{2,0,1:T(8,128)(2,1)}, u32[]{:S(2)}, u32[]{:S(2)}) async-start(bf16[16,2,131072]{2,0,1:T(8,128)(2,1)} %copy.95), calls=%async_computation.5 | async-start | bytes 16777216 | tf_op jit(solution)/shard_map/all_to_all | solution.py:349
  903.8 419.2 %all-reduce.13.cloned.1.call-start = ((), (), s32[]{:S(2)}) async-start(), calls=%async_computation.15 | async-start | bytes 34308096
  1004.3 15.7 %all-to-all-start.7 = ((bf16[16,2,384]{2,0,1:T(8,128)(2,1)}), bf16[16,2,384]{2,0,1:T(8,128)(2,1)S(1)}, u32[]{:S(2)}, u32[]{:S(2)}) async-start(bf16[16,2,384]{2,0,1:T(8,128)(2,1)} %copy.97), calls=%async_computation.7 | async-start | bytes 49152 | tf_op jit(solution)/shard_map/all_to_all | solution.py:355
  1014.6 324.4 %copy-start.1 = (bf16[1,48,4,128]{3,2,1,0:T(4,128)(2,1)S(1)}, bf16[1,48,4,128]{3,2,1,0:T(4,128)(2,1)}, u32[]{:S(2)}) copy-start(bf16[1,48,4,128]{3,2,1,0:T(4,128)(2,1)} %param.13) | copy-start | bytes 147460
  (51 other events, 392.7 us)
Sparse Core Ops, SparseCore 0:
  11.0 56.6 all-gather.10
  70.7 55.7 all-gather.14
  129.4 73.6 all-gather.8
  205.8 68.8 all-gather.12
  277.6 75.5 all-gather.16
  356.0 75.7 all-gather.18
  998.7 324.2 all-reduce.12
where the time goes:
time: 1360 us; the launch traced here: 1350 us
  waiting for transfers between devices  393 us (29%)
  local copies, waits for them, and re-layouts  312 us (23%)
  blocking collectives  272 us (20%)
  matrix products  199 us (15%)
  other arithmetic  108 us (8%)
  starting transfers between devices  47.3 us (3%)
  between operations  15.6 us (1%)
    unnamed x8, waiting for transfers between devices  229 us
    unnamed x1, blocking collectives  76.5 us
    all_gather x1, blocking collectives, on_device(): lax.all_gather(embed_table, ('wide', 'narrow'), axis=0, tiled=True)  73.9 us
    all_gather x1, blocking collectives, on_device(): lax.all_gather(positions, ('wide', 'narrow'), axis=0, tiled=True)  64.8 us
    reshape x2, local copies, waits for them, and re-layouts, on_device(): slot_keys = key_value[:, :D].reshape(VARS, length, HEADS, head_size)  59.9 us
    all_to_all x1, waiting for transfers between devices, on_device(): lax.all_to_all(block_mlp_in.astype(jnp.bfloat16), 'narrow', split_axis=1,...  56.9 us
    all_gather x1, blocking collectives, on_device(): lax.all_gather(vectors, ('wide', 'narrow'), axis=0, tiled=True)  56.4 us
    all_to_all x1, waiting for transfers between devices, on_device(): lax.all_to_all(block_mlp_out.astype(jnp.bfloat16), 'narrow', split_axis=1...  55 us
  transfers between devices with their start and end apart: 16, of which 6 were waited for; matrix products, arithmetic and copies ran while one was open for 34% of the time, Pallas kernels for 0%

commit v1 on v0

--- a/solution.py
+++ b/solution.py
@@ -90,44 +90,30 @@
     length = PATCHES
     single_float = jnp.float32
     bf16 = jnp.bfloat16
-    pixel_values = fields[0]
     onehot = (var_ids[0][:, None] == jnp.arange(VARS)[None, :]).astype(bf16)
-    slot_lookup_table = jnp.dot(onehot, table_full, preferred_element_type=single_float).reshape(
-        VARS, PATCH_PIXELS + 1, D
-    )
-    patch_row_block = slot_lookup_table[:, :PATCH_PIXELS].astype(bf16)
-    token_rows = (
-        jnp.einsum(
-            "tnz,tnu->tzu", pixel_values, patch_row_block, preferred_element_type=single_float
-        )
-        + slot_lookup_table[:, PATCH_PIXELS][:, None, :]
-    )
-    token_rows = token_rows.astype(bf16)
+    var_pixels = jnp.einsum("sv,spl->pvl", onehot, fields[0], preferred_element_type=single_float)
+    live = jnp.einsum("sv,s->v", onehot, slot_mask[0].astype(bf16), preferred_element_type=single_float)
+    pixels = jnp.concatenate([var_pixels, jnp.ones((1, VARS, length), single_float)], 0)
+    table_rows = table_full.reshape(VARS, PATCH_PIXELS + 1, D).transpose(1, 0, 2).reshape(-1, D)
     query_row = vector_rows[0]
     agg_query = jnp.dot(
         query_row[None, :], agg_in_full[:, :D], preferred_element_type=single_float
     )[0].astype(bf16)
-    flat_tokens = token_rows.reshape(VARS * length, D)
-    key_value = jnp.dot(
-        flat_tokens, agg_in_full[:, D:], preferred_element_type=single_float
-    ).astype(bf16)
-    slot_keys = key_value[:, :D].reshape(VARS, length, HEADS, head_size)
-    slot_values = key_value[:, D:].reshape(VARS, length, HEADS, head_size)
-    live_slots = slot_mask[0] > 0
-    agg_scores = (
-        jnp.einsum(
-            "hc,slhc->lhs",
-            agg_query.reshape(HEADS, head_size),
-            slot_keys,
-            preferred_element_type=single_float,
-        )
-        * score_scale
-    )
-    agg_scores = jnp.where(live_slots[None, None, :], agg_scores, masked_score)
-    agg_probs = softmax_rows(agg_scores)
-    agg_probs_low = agg_probs.astype(bf16)
+    table_kv = jnp.dot(table_rows, agg_in_full[:, D:], preferred_element_type=single_float)
+    table_keys = table_kv[:, :D]
+    table_values = table_kv[:, D:].astype(bf16).reshape(-1, HEADS, head_size)
+    query_wide = agg_query.astype(single_float)
+    key_dots = (
+        jnp.sum((table_keys * query_wide).reshape(-1, HEADS, head_size), -1) * score_scale
+    ).reshape(PATCH_PIXELS + 1, VARS, HEADS).transpose(0, 2, 1)
+    agg_scores = jnp.sum(pixels[:, None] * key_dots[..., None], 0)
+    agg_scores = jnp.where(live[None, :, None] > 0, agg_scores, masked_score)
+    score_top = jnp.max(agg_scores, 1, keepdims=True)
+    agg_expo = jnp.exp(agg_scores - score_top)
+    agg_probs = agg_expo / jnp.sum(agg_expo, 1, keepdims=True)
+    spread = (agg_probs[:, None] * pixels[None]).astype(bf16).reshape(HEADS, -1, length)
     mixture = (
-        jnp.einsum("lhs,slhc->lhc", agg_probs_low, slot_values, preferred_element_type=single_float)
+        jnp.einsum("hrl,rhc->lhc", spread, table_values, preferred_element_type=single_float)
         .reshape(length, D)
         .astype(bf16)
     )
@@ -168,28 +154,6 @@
         + jnp.dot(activated, mlp_out_full, preferred_element_type=single_float)
         + row_values[7]
     ).astype(bf16)
-    regathered = (
-        lax.all_gather(embed_table, ("wide", "narrow"), axis=0, tiled=True),
-        lax.all_gather(agg_in, ("wide", "narrow"), axis=0, tiled=True),
-        lax.all_gather(agg_out, ("wide", "narrow"), axis=0, tiled=True),
-        lax.all_gather(attn_in, ("wide", "narrow"), axis=0, tiled=True),
-        lax.all_gather(attn_out, ("wide", "narrow"), axis=0, tiled=True),
-        lax.all_gather(mlp_in, ("wide", "narrow"), axis=0, tiled=True),
-        lax.all_gather(mlp_out, ("wide", "narrow"), axis=0, tiled=True),
-        lax.all_gather(vectors, ("wide", "narrow"), axis=0, tiled=True),
-        lax.all_gather(positions, ("wide", "narrow"), axis=0, tiled=True),
-    )
-    (
-        table_full,
-        agg_in_full,
-        agg_out_full,
-        attn_in_full,
-        attn_out_full,
-        mlp_in_full,
-        mlp_out_full,
-        vector_rows,
-        position_rows,
-    ) = unpack(regathered)
     grad_output = cotangent[0].astype(single_float)
     grad_branch2 = grad_output.astype(bf16)
     grad_fc2_bias = jnp.sum(grad_branch2.astype(single_float), 0)
@@ -254,53 +218,41 @@
         .astype(bf16)
         .reshape(length, HEADS, head_size)
     )
-    grad_agg_probs = jnp.einsum(
-        "lhc,slhc->lhs", grad_mixture, slot_values, preferred_element_type=single_float
-    )
-    grad_agg_scores = (
-        agg_probs * (grad_agg_probs - jnp.sum(agg_probs * grad_agg_probs, -1, keepdims=True))
-    ).astype(bf16)
-    grad_slot_values = jnp.einsum(
-        "lhs,lhc->slhc", agg_probs_low, grad_mixture, preferred_element_type=single_float
-    )
-    grad_slot_keys = (
-        jnp.einsum(
-            "lhs,hc->slhc",
-            grad_agg_scores,
-            agg_query.reshape(HEADS, head_size),
-            preferred_element_type=single_float,
-        )
-        * score_scale
-    )
-    grad_agg_query = (
-        jnp.einsum("lhs,slhc->hc", grad_agg_scores, slot_keys, preferred_element_type=single_float)
-        * score_scale
-    ).reshape(D)
-    grad_key_value = jnp.concatenate(
-        [grad_slot_keys.reshape(VARS * length, D), grad_slot_values.reshape(VARS * length, D)], 1
-    ).astype(bf16)
-    grad_agg_kv = jnp.dot(flat_tokens.T, grad_key_value, preferred_element_type=single_float)
-    grad_token_rows = (
-        jnp.dot(grad_key_value, agg_in_full[:, D:].T, preferred_element_type=single_float)
-        .astype(bf16)
-        .reshape(VARS, length, D)
+    back_mix = jnp.einsum(
+        "rhc,lhc->hrl", table_values, grad_mixture, preferred_element_type=single_float
+    ).reshape(HEADS, PATCH_PIXELS + 1, VARS, length)
+    grad_agg_probs = jnp.sum(back_mix * pixels[None], 1)
+    grad_agg_scores = agg_probs * (
+        grad_agg_probs - jnp.sum(agg_probs * grad_agg_probs, 1, keepdims=True)
+    )
+    grad_pixels = jnp.sum(
+        grad_agg_scores[:, None] * key_dots.transpose(1, 0, 2)[..., None]
+        + agg_probs[:, None] * back_mix,
+        0,
+    )[:PATCH_PIXELS].astype(bf16)
+    fields_grad = jnp.einsum(
+        "sv,pvl->spl", onehot, grad_pixels, preferred_element_type=single_float
+    ).astype(bf16)
+    grad_dots = (
+        jnp.sum(pixels[None] * grad_agg_scores[:, None], -1) * score_scale
+    ).reshape(HEADS, -1).T
+    grad_table_values = jnp.einsum(
+        "hrl,lhc->rhc", spread, grad_mixture, preferred_element_type=single_float
+    ).reshape(-1, D)
+    dots_wide = jnp.repeat(grad_dots, head_size, 1)
+    grad_agg_query = jnp.sum(dots_wide * table_keys, 0)
+    grad_table_kv = jnp.concatenate([dots_wide * query_wide, grad_table_values], 1).astype(bf16)
+    grad_agg_kv = jnp.dot(table_rows.T, grad_table_kv, preferred_element_type=single_float)
+    grad_table = (
+        jnp.dot(grad_table_kv, agg_in_full[:, D:].T, preferred_element_type=single_float)
+        .reshape(PATCH_PIXELS + 1, VARS, D)
+        .transpose(1, 0, 2)
     )
     grad_agg_qproj = query_row.astype(single_float)[:, None] * grad_agg_query[None, :]
     grad_query_row = jnp.dot(
         agg_in_full[:, :D].astype(single_float), grad_agg_query, precision=highest_precision
     )
     grad_agg_in = jnp.concatenate([grad_agg_qproj, grad_agg_kv], 1)
-    grad_patch_rows = jnp.einsum(
-        "hzo,how->hzw", pixel_values, grad_token_rows, preferred_element_type=single_float
-    )
-    grad_embed = jnp.sum(grad_token_rows.astype(single_float), 1)
-    grad_slots = jnp.concatenate([grad_patch_rows, grad_embed[:, None, :]], 1).reshape(
-        VARS, (PATCH_PIXELS + 1) * D
-    )
-    grad_table = jnp.dot(onehot.astype(single_float).T, grad_slots, precision=highest_precision)
-    fields_grad = jnp.einsum(
-        "cyi,cgi->cgy", grad_token_rows, patch_row_block, preferred_element_type=single_float
-    ).astype(bf16)
     grad_rows = jnp.concatenate(
         [
             jnp.stack(
@@ -319,75 +271,19 @@
         ],
         0,
     )
-    wide_count = lax.axis_size("wide")
-    narrow_count = lax.axis_size("narrow")
-    block_table = grad_table.reshape(wide_count, narrow_count, -1)
-    block_agg_in = grad_agg_in.reshape(wide_count, narrow_count, -1)
-    block_agg_out = grad_agg_out.reshape(wide_count, narrow_count, -1)
-    block_attn_in = grad_attn_in.reshape(wide_count, narrow_count, -1)
-    block_attn_out = grad_attn_out.reshape(wide_count, narrow_count, -1)
-    block_mlp_in = grad_mlp_in.reshape(wide_count, narrow_count, -1)
-    block_mlp_out = grad_mlp_out.reshape(wide_count, narrow_count, -1)
-    block_rows = grad_rows.reshape(wide_count, narrow_count, -1)
-    block_positions = grad_stream.reshape(wide_count, narrow_count, -1)
-    regrouped = (
-        lax.all_to_all(
-            block_table.astype(jnp.bfloat16), "narrow", split_axis=1, concat_axis=1, tiled=True
-        ).astype(block_table.dtype),
-        lax.all_to_all(
-            block_agg_in.astype(jnp.bfloat16), "narrow", split_axis=1, concat_axis=1, tiled=True
-        ).astype(block_agg_in.dtype),
-        lax.all_to_all(
-            block_agg_out.astype(jnp.bfloat16), "narrow", split_axis=1, concat_axis=1, tiled=True
-        ).astype(block_agg_out.dtype),
-        lax.all_to_all(
-            block_attn_in.astype(jnp.bfloat16), "narrow", split_axis=1, concat_axis=1, tiled=True
-        ).astype(block_attn_in.dtype),
-        lax.all_to_all(
-            block_attn_out.astype(jnp.bfloat16), "narrow", split_axis=1, concat_axis=1, tiled=True
-        ).astype(block_attn_out.dtype),
-        lax.all_to_all(
-            block_mlp_in.astype(jnp.bfloat16), "narrow", split_axis=1, concat_axis=1, tiled=True
-        ).astype(block_mlp_in.dtype),
-        lax.all_to_all(
-            block_mlp_out.astype(jnp.bfloat16), "narrow", split_axis=1, concat_axis=1, tiled=True
-        ).astype(block_mlp_out.dtype),
-        lax.all_to_all(
-            block_rows.astype(jnp.bfloat16), "narrow", split_axis=1, concat_axis=1, tiled=True
-        ).astype(block_rows.dtype),
-        lax.all_to_all(
-            block_positions.astype(jnp.bfloat16), "narrow", split_axis=1, concat_axis=1, tiled=True
-        ).astype(block_positions.dtype),
-    )
-    partial_sums = tuple((jnp.sum(member, 1) for member in regrouped))
-    summed = (
-        lax.psum_scatter(
-            partial_sums[0].astype(jnp.bfloat16), "wide", scatter_dimension=0, tiled=True
-        ).astype(jnp.float32),
-        lax.psum_scatter(
-            partial_sums[1].astype(jnp.bfloat16), "wide", scatter_dimension=0, tiled=True
-        ).astype(jnp.float32),
-        lax.psum_scatter(
-            partial_sums[2].astype(jnp.bfloat16), "wide", scatter_dimension=0, tiled=True
-        ).astype(jnp.float32),
-        lax.psum_scatter(
-            partial_sums[3].astype(jnp.bfloat16), "wide", scatter_dimension=0, tiled=True
-        ).astype(jnp.float32),
-        lax.psum_scatter(
-            partial_sums[4].astype(jnp.bfloat16), "wide", scatter_dimension=0, tiled=True
-        ).astype(jnp.float32),
-        lax.psum_scatter(
-            partial_sums[5].astype(jnp.bfloat16), "wide", scatter_dimension=0, tiled=True
-        ).astype(jnp.float32),
-        lax.psum_scatter(
-            partial_sums[6].astype(jnp.bfloat16), "wide", scatter_dimension=0, tiled=True
-        ).astype(jnp.float32),
-        lax.psum_scatter(
-            partial_sums[7].astype(jnp.bfloat16), "wide", scatter_dimension=0, tiled=True
-        ).astype(jnp.float32),
-        lax.psum_scatter(
-            partial_sums[8].astype(jnp.bfloat16), "wide", scatter_dimension=0, tiled=True
-        ).astype(jnp.float32),
+    parts = (
+        grad_table, grad_agg_in, grad_agg_out, grad_attn_in, grad_attn_out,
+        grad_mlp_in, grad_mlp_out, grad_rows, grad_stream,
+    )
+    devices = lax.axis_size("wide") * lax.axis_size("narrow")
+    summed = tuple(
+        jnp.sum(
+            lax.all_to_all(
+                part.astype(bf16).reshape(devices, -1), ("wide", "narrow"), 0, 0, tiled=True
+            ).astype(single_float),
+            0,
+        )
+        for part in parts
     )
     return (
         result[None],

time: 1360 us -> 1440 us (1.059)
  other arithmetic: 108 us -> 320 us
  matrix products: 199 us -> 84.9 us
  blocking collectives: 272 us -> 196 us
  local copies, waits for them, and re-layouts: 312 us -> 379 us
  waiting for transfers between devices: 393 us -> 373 us
    unnamed x8 -> x6, waiting for transfers between devices: 229 us -> 3.64 us
    all_to_all x0 -> x7, other arithmetic: none -> 179 us  [on_device(): lax.all_to_all(part.astype(bf16).reshape(devices, -1), ('wide', 'narrow')...]
    unnamed x141 -> x112, local copies, waits for them, and re-layouts: 32.4 us -> 179 us
    dot_general x10 -> x9, matrix products: 135 us -> 15.8 us  [the longest x1 3.77 us: on_device(): jnp.dot(grad_table_kv, agg_in_full[:, D:].T, preferred_element_type=singl...]
    all_to_all x0 -> x8, local copies, waits for them, and re-layouts: none -> 96.5 us  [on_device(): lax.all_to_all(part.astype(bf16).reshape(devices, -1), ('wide', 'narrow')...]
    convert_element_type x20 -> x3, local copies, waits for them, and re-layouts: 112 us -> 22.4 us  [on_device(): part.astype(bf16).reshape(devices, -1)]
    unnamed x1 -> x0, blocking collectives: 76.5 us -> none
    all_to_all x9, waiting for transfers between devices: 164 us -> 225 us  [on_device(): lax.all_to_all(part.astype(bf16).reshape(devices, -1), ('wide', 'narrow')...]
  transfers between devices with their start and end apart: 16 -> 15, of which waited for: 6 -> 8; matrix products, arithmetic and copies ran while one was open for 34% -> 41% of each run, Pallas kernels for 0% -> 0%
where the time goes in v1:
time: 1440 us; the launch traced here: 1420 us
  local copies, waits for them, and re-layouts  379 us (26%)
  waiting for transfers between devices  373 us (26%)
  other arithmetic  320 us (22%)
  blocking collectives  196 us (14%)
  matrix products  84.9 us (6%)
  starting transfers between devices  56.7 us (4%)
  between operations  15.5 us (1%)
    all_to_all x9, waiting for transfers between devices, on_device(): lax.all_to_all(part.astype(bf16).reshape(devices, -1), ('wide', 'narrow')...  225 us
    unnamed x112, local copies, waits for them, and re-layouts  179 us
    all_to_all x7, other arithmetic, on_device(): lax.all_to_all(part.astype(bf16).reshape(devices, -1), ('wide', 'narrow')...  179 us
    all_to_all x8, local copies, waits for them, and re-layouts, on_device(): lax.all_to_all(part.astype(bf16).reshape(devices, -1), ('wide', 'narrow')...  96.5 us
    reduce_sum x9, other arithmetic, on_device(): jnp.sum(lax.all_to_all(part.astype(bf16).reshape(devices, -1), ('wide', '...  80.3 us
    all_gather x1, blocking collectives, on_device(): lax.all_gather(embed_table, ('wide', 'narrow'), axis=0, tiled=True)  74.1 us
    all_gather x1, blocking collectives, on_device(): lax.all_gather(positions, ('wide', 'narrow'), axis=0, tiled=True)  65.6 us
    all_gather x1, waiting for transfers between devices, on_device(): lax.all_gather(mlp_out, ('wide', 'narrow'), axis=0, tiled=True)  60.3 us
  transfers between devices with their start and end apart: 15, of which 8 were waited for; matrix products, arithmetic and copies ran while one was open for 41% of the time, Pallas kernels for 0%

profile of v1, /device:TPU:8, one launch (start us, length us, event | category | flops | bytes accessed | tf_op | source)
XLA Modules:
  0.0 1424.2 jit_solution(4013927213627634305)
XLA Ops:
  13.6 55.9 %all-gather.1 = bf16[32,1,384]{2,1,0:T(2,128)(2,1)S(1)} all-gather(bf16[1,1,384]{2,1,0:T(2,128)(2,1)S(1)} %reshape.352), channel_id=1, replica_groups=mesh['wide'=16,'narrow'=2] {'wide','narrow'}, dimensions={0}, use_global_device_ids=true | all-gather | bytes 25344 | tf_op jit(solution)/shard_map/all_gather | solution.py:74
  69.7 65.6 %all_gather.31 = bf16[131072]{0:T(1024)(128)(2,1)S(1)} all-gather(bf16[4096]{0:T(1024)(128)(2,1)} %param.24), channel_id=1, replica_groups=mesh['wide'=16,'narrow'=2] {'wide','narrow'}, dimensions={0}, use_global_device_ids=true | all-gather | bytes 270336 | tf_op jit(solution)/shard_map/all_gather | solution.py:75
  135.4 74.1 %all-gather = bf16[32,1,7680]{2,1,0:T(2,128)(2,1)S(1)} all-gather(bf16[1,1,7680]{2,1,0:T(2,128)(2,1)S(1)} %reshape.350), channel_id=1, replica_groups=mesh['wide'=16,'narrow'=2] {'wide','narrow'}, dimensions={0}, use_global_device_ids=true | all-gather | bytes 506880 | tf_op jit(solution)/shard_map/all_gather | solution.py:67
  250.2 26.1 %all-gather.13.cloned.1.call-done = bf16[3145728]{0:T(1024)(128)(2,1)} async-done(((bf16[98304]{0:T(1024)(128)(2,1)}), bf16[3145728]{0:T(1024)(128)(2,1)}) %all-gather.13.cloned.1.call-update) | async-done | bytes 6291472 | tf_op jit(solution)/shard_map/all_gather | solution.py:70
  296.8 58.0 %all-gather.17.cloned.1.call-done = bf16[4194304]{0:T(1024)(128)(2,1)} async-done(((bf16[131072]{0:T(1024)(128)(2,1)}), bf16[4194304]{0:T(1024)(128)(2,1)}) %all-gather.17.cloned.1.call-update) | async-done | bytes 8388624 | tf_op jit(solution)/shard_map/all_gather | solution.py:72
  354.8 13.4 reshape.332
  373.1 60.3 %all-gather.19.cloned.1.call-done = bf16[4194304]{0:T(1024)(128)(2,1)} async-done(((bf16[131072]{0:T(1024)(128)(2,1)}), bf16[4194304]{0:T(1024)(128)(2,1)}) %all-gather.19.cloned.1.call-update) | async-done | bytes 8388624 | tf_op jit(solution)/shard_map/all_gather | solution.py:73
  433.4 13.7 reshape.333
  552.6 14.5 %reduce.25 = bf16[32,32768]{1,0:T(8,128)(2,1)} reduce(bf16[32,1,32768]{2,1,0:T(2,128)(2,1)} %all_to_all.69, bf16[]{:T(256)} %broadcast.226), dimensions={1}, to_apply=%all_to_all.69.reduce_sub_computation | reduce | bytes 4194306 | tf_op jit(solution)/shard_map/all_to_all | solution.py:281
  590.9 14.5 %reduce.23 = bf16[32,32768]{1,0:T(8,128)(2,1)} reduce(bf16[32,1,32768]{2,1,0:T(2,128)(2,1)} %all_to_all.67, bf16[]{:T(256)} %broadcast.226), dimensions={1}, to_apply=%all_to_all.67.reduce_sub_computation | reduce | bytes 4194306 | tf_op jit(solution)/shard_map/all_to_all | solution.py:281
  609.9 14.1 all-to-all-done.4
  636.2 21.1 %all_to_all.68 = bf16[32,1,98304]{2,1,0:T(2,128)(2,1)} reshape(bf16[1024,3072]{1,0:T(8,128)(2,1)} %convolution_convert_fusion.2) | data formatting | bytes 12582912 | tf_op jit(solution)/shard_map/all_to_all | solution.py:281
  657.3 39.4 %reduce.24 = bf16[32,98304]{1,0:T(8,128)(2,1)} reduce(bf16[32,1,98304]{2,1,0:T(2,128)(2,1)} %all_to_all.68, bf16[]{:T(256)} %broadcast.226), dimensions={1}, to_apply=%all_to_all.68.reduce_sub_computation | reduce | bytes 12582914 | tf_op jit(solution)/shard_map/all_to_all | solution.py:281
  726.7 21.1 %convert_element_type.258 = bf16[32,1,98304]{2,1,0:T(2,128)(2,1)} reshape(bf16[1024,3072]{1,0:T(8,128)(2,1)} %copy.166) | data formatting | bytes 12582912 | tf_op jit(solution)/shard_map/convert_element_type | solution.py:282
  747.9 39.3 %reduce.22 = bf16[32,98304]{1,0:T(8,128)(2,1)} reduce(bf16[32,1,98304]{2,1,0:T(2,128)(2,1)} %convert_element_type.258, bf16[]{:T(256)} %broadcast.226), dimensions={1}, to_apply=%convert_element_type.258.reduce_sub_computation | reduce | bytes 12582914 | tf_op jit(solution)/shard_map/convert_element_type | solution.py:282
  795.9 53.6 %all-to-all-done.3 = bf16[32,2,49152]{2,1,0:T(2,128)(2,1)} async-done(((bf16[32,2,49152]{2,1,0:T(2,128)(2,1)}), bf16[32,2,49152]{2,1,0:T(2,128)(2,1)}, u32[]{:S(2)}, u32[]{:S(2)}) %all-to-all-start.3) | async-done | bytes 6291488 | tf_op jit(solution)/shard_map/all_to_all | solution.py:281
  863.6 26.2 %all_to_all.70 = bf16[32,1,131072]{2,1,0:T(2,128)(2,1)} reshape(bf16[1024,4096]{1,0:T(8,128)(2,1)} %convolution_convert_fusion.1) | data formatting | bytes 16777216 | tf_op jit(solution)/shard_map/all_to_all | solution.py:281
  889.9 50.4 %reduce.26 = bf16[32,131072]{1,0:T(8,128)(2,1)} reduce(bf16[32,1,131072]{2,1,0:T(2,128)(2,1)} %all_to_all.70, bf16[]{:T(256)} %broadcast.226), dimensions={1}, to_apply=%all_to_all.70.reduce_sub_computation | reduce | bytes 16777218 | tf_op jit(solution)/shard_map/all_to_all | solution.py:281
  940.3 10.9 reshape.375
  951.2 43.0 %all-to-all-done.1 = bf16[32,2,49152]{2,1,0:T(2,128)(2,1)} async-done(((bf16[32,2,49152]{2,1,0:T(2,128)(2,1)}), bf16[32,2,49152]{2,1,0:T(2,128)(2,1)}, u32[]{:S(2)}, u32[]{:S(2)}) %all-to-all-start.1) | async-done | bytes 6291488 | tf_op jit(solution)/shard_map/all_to_all | solution.py:281
  1006.0 22.7 %all_to_all.71 = bf16[32,1,131072]{2,1,0:T(2,128)(2,1)} reshape(bf16[4096,1024]{1,0:T(8,128)(2,1)} %convolution_convert_fusion) | data formatting | bytes 16777216 | tf_op jit(solution)/shard_map/all_to_all | solution.py:281
  1028.7 50.4 %reduce.27 = bf16[32,131072]{1,0:T(8,128)(2,1)} reduce(bf16[32,1,131072]{2,1,0:T(2,128)(2,1)} %all_to_all.71, bf16[]{:T(256)} %broadcast.226), dimensions={1}, to_apply=%all_to_all.71.reduce_sub_computation | reduce | bytes 16777218 | tf_op jit(solution)/shard_map/all_to_all | solution.py:281
  1090.1 94.4 %all-to-all-done.5 = bf16[32,2,65536]{2,1,0:T(2,128)(2,1)} async-done(((bf16[32,2,65536]{2,1,0:T(2,128)(2,1)}), bf16[32,2,65536]{2,1,0:T(2,128)(2,1)}, u32[]{:S(2)}, u32[]{:S(2)}) %all-to-all-start.5) | async-done | bytes 8388640 | tf_op jit(solution)/shard_map/all_to_all | solution.py:281
  1243.6 21.6 %reshape.372 = bf16[32,1,98304]{2,1,0:T(2,128)(2,1)} reshape(bf16[32,2,49152]{2,1,0:T(2,128)(2,1)} %all-to-all-done.3) | data formatting | bytes 12582912
  1265.2 21.6 %reshape.368 = bf16[32,1,98304]{2,1,0:T(2,128)(2,1)} reshape(bf16[32,2,49152]{2,1,0:T(2,128)(2,1)} %all-to-all-done.1) | data formatting | bytes 12582912
  1286.9 14.1 convert_reduce_fusion.2
  1301.0 13.1 convert_reduce_fusion.3
  1314.1 23.4 %reshape.376 = bf16[32,1,131072]{2,1,0:T(2,128)(2,1)} reshape(bf16[32,2,65536]{2,1,0:T(2,128)(2,1)} %all-to-all-done.5) | data formatting | bytes 16777216
  1337.5 18.1 %convert_reduce_fusion.1 = f32[131072]{0:T(1024)} fusion(bf16[32,1,131072]{2,1,0:T(2,128)(2,1)} %reshape.376), kind=kLoop, calls=%fused_computation.2 | loop fusion | flops 8257536 | bytes 8912896 | tf_op jit(solution)/shard_map/reduce_sum | solution.py:280
  1355.5 20.0 %all-to-all-done.6 = bf16[32,2,65536]{2,1,0:T(2,128)(2,1)} async-done(((bf16[32,2,65536]{2,1,0:T(2,128)(2,1)}), bf16[32,2,65536]{2,1,0:T(2,128)(2,1)}, u32[]{:S(2)}, u32[]{:S(2)}) %all-to-all-start.6) | async-done | bytes 8388640 | tf_op jit(solution)/shard_map/all_to_all | solution.py:281
  1375.5 23.4 %reshape.378 = bf16[32,1,131072]{2,1,0:T(2,128)(2,1)} reshape(bf16[32,2,65536]{2,1,0:T(2,128)(2,1)} %all-to-all-done.6) | data formatting | bytes 16777216
  1398.9 18.1 %convert_reduce_fusion = f32[131072]{0:T(1024)} fusion(bf16[32,1,131072]{2,1,0:T(2,128)(2,1)} %reshape.378), kind=kLoop, calls=%fused_computation.1 | loop fusion | flops 8257536 | bytes 8912896 | tf_op jit(solution)/shard_map/reduce_sum | solution.py:280
  (260 shorter events, 352.4 us)
Async XLA Ops:
  7.2 207.6 %copy-start = (bf16[1,48,4,128]{3,2,1,0:T(4,128)(2,1)S(1)}, bf16[1,48,4,128]{3,2,1,0:T(4,128)(2,1)}, u32[]{:S(2)}) copy-start(bf16[1,48,4,128]{3,2,1,0:T(4,128)(2,1)} %param.13) | copy-start | bytes 147460
  7.2 208.1 %all-gather.11.cloned.1.call-start = ((), (), s32[]{:S(2)}) async-start(), calls=%async_computation.10 | async-start | bytes 2162688 | tf_op jit(solution)/shard_map/all_gather | solution.py:69
  7.9 210.4 %all-gather.15.cloned.1.call-start = ((), (), s32[]{:S(2)}) async-start(), calls=%async_computation.12 | async-start | bytes 2162688 | tf_op jit(solution)/shard_map/all_gather | solution.py:71
  8.7 214.3 %all-gather.9.cloned.1.call-start = ((), (), s32[]{:S(2)}) async-start(), calls=%async_computation.9 | async-start | bytes 6488064 | tf_op jit(solution)/shard_map/all_gather | solution.py:68
  9.4 266.9 %all-gather.13.cloned.1.call-start = ((), (), s32[]{:S(2)}) async-start(), calls=%async_computation.11 | async-start | bytes 6488064 | tf_op jit(solution)/shard_map/all_gather | solution.py:70
  10.0 344.8 %all-gather.17.cloned.1.call-start = ((), (), s32[]{:S(2)}) async-start(), calls=%async_computation.13 | async-start | bytes 8650752 | tf_op jit(solution)/shard_map/all_gather | solution.py:72
  10.6 422.8 %all-gather.19.cloned.1.call-start = ((), (), s32[]{:S(2)}) async-start(), calls=%async_computation.14 | async-start | bytes 8650752 | tf_op jit(solution)/shard_map/all_gather | solution.py:73
  215.1 33.2 %copy-start.27 = (f32[5,48,128]{2,1,0:T(8,128)}, f32[5,48,128]{2,1,0:T(8,128)S(1)}, u32[]{:S(2)}) copy-start(f32[5,48,128]{2,1,0:T(8,128)S(1)} %concatenate.22) | copy-start | bytes 368644
  218.3 70.0 %copy-start.9 = (bf16[1024,1024]{1,0:T(8,128)(2,1)}, bf16[1024,1024]{1,0:T(8,128)(2,1)S(1)}, u32[]{:S(2)}) copy-start(bf16[1024,1024]{1,0:T(8,128)(2,1)S(1)} %reshape.326) | copy-start | bytes 6291460
  223.0 10.4 copy-start.40
  240.0 46.6 %copy-start.17 = (bf16[240,1024]{0,1:T(8,128)(2,1)}, bf16[240,1024]{0,1:T(8,128)(2,1)S(1)}, u32[]{:S(2)}) copy-start(bf16[240,1024]{0,1:T(8,128)(2,1)S(1)} %copy.147) | copy-start | bytes 1474564
  247.5 39.1 %copy-start.37 = (f32[5,48,16]{1,0,2:T(8,128)}, f32[5,48,16]{1,0,2:T(8,128)S(1)}, u32[]{:S(2)}) copy-start(f32[5,48,16]{1,0,2:T(8,128)S(1)} %mul.308) | copy-start | bytes 46084
  294.5 73.7 %copy-start.30 = (bf16[16,64,128]{2,1,0:T(8,128)(2,1)}, bf16[16,64,128]{2,1,0:T(8,128)(2,1)S(1)}, u32[]{:S(2)}) copy-start(bf16[16,64,128]{2,1,0:T(8,128)(2,1)S(1)} %convolution_convert_fusion.9) | copy-start | bytes 786436
  373.1 74.0 %copy-start.20 = (bf16[1,128,1024]{2,1,0:T(8,128)(2,1)S(1)}, bf16[1,128,1024]{2,1,0:T(8,128)(2,1)}, u32[]{:S(2)}) copy-start(bf16[1,128,1024]{2,1,0:T(8,128)(2,1)} %param.25) | copy-start | bytes 786436
  447.1 8.0 copy-start.2
  447.1 8.0 copy-start.5
  469.5 7.7 copy-start.19
  495.4 11.1 all-to-all-start.7
  506.5 26.5 %all-to-all-start.8 = ((bf16[32,2,2048]{2,1,0:T(2,128)(2,1)}), bf16[32,2,2048]{2,1,0:T(2,128)(2,1)}, u32[]{:S(2)}, u32[]{:S(2)}) async-start(bf16[32,2,2048]{2,1,0:T(2,128)(2,1)} %reshape.381), calls=%async_computation.8 | async-start | bytes 524288 | tf_op jit(solution)/shard_map/all_to_all | solution.py:281
  533.0 38.6 %all-to-all-start = ((bf16[32,2,3840]{2,1,0:T(2,128)(2,1)}), bf16[32,2,3840]{2,1,0:T(2,128)(2,1)}, u32[]{:S(2)}, u32[]{:S(2)}) async-start(bf16[32,2,3840]{2,1,0:T(2,128)(2,1)} %reshape.365), calls=%async_computation | async-start | bytes 983040 | tf_op jit(solution)/shard_map/all_to_all | solution.py:281
  571.6 52.4 %all-to-all-start.4 = ((bf16[32,2,16384]{2,1,0:T(2,128)(2,1)}), bf16[32,2,16384]{2,1,0:T(2,128)(2,1)}, u32[]{:S(2)}, u32[]{:S(2)}) async-start(bf16[32,2,16384]{2,1,0:T(2,128)(2,1)} %reshape.373), calls=%async_computation.4 | async-start | bytes 4194304 | tf_op jit(solution)/shard_map/all_to_all | solution.py:281
  624.0 81.5 %all-to-all-start.2 = ((bf16[32,2,16384]{2,1,0:T(2,128)(2,1)}), bf16[32,2,16384]{2,1,0:T(2,128)(2,1)}, u32[]{:S(2)}, u32[]{:S(2)}) async-start(bf16[32,2,16384]{2,1,0:T(2,128)(2,1)} %reshape.369), calls=%async_computation.2 | async-start | bytes 4194304 | tf_op jit(solution)/shard_map/all_to_all | solution.py:281
  705.5 144.0 %all-to-all-start.3 = ((bf16[32,2,49152]{2,1,0:T(2,128)(2,1)}), bf16[32,2,49152]{2,1,0:T(2,128)(2,1)}, u32[]{:S(2)}, u32[]{:S(2)}) async-start(bf16[32,2,49152]{2,1,0:T(2,128)(2,1)} %reshape.371), calls=%async_computation.3 | async-start | bytes 12582912 | tf_op jit(solution)/shard_map/all_to_all | solution.py:281
  795.9 60.8 %copy-start.6 = (f32[128,1024]{1,0:T(8,128)S(1)}, f32[128,1024]{1,0:T(8,128)}, u32[]{:S(2)}) copy-start(f32[128,1024]{1,0:T(8,128)} %copy-done.4) | copy-start | bytes 1572868
  849.6 144.6 %all-to-all-start.1 = ((bf16[32,2,49152]{2,1,0:T(2,128)(2,1)}), bf16[32,2,49152]{2,1,0:T(2,128)(2,1)}, u32[]{:S(2)}, u32[]{:S(2)}) async-start(bf16[32,2,49152]{2,1,0:T(2,128)(2,1)} %reshape.367), calls=%async_computation.1 | async-start | bytes 12582912 | tf_op jit(solution)/shard_map/all_to_all | solution.py:281
  994.2 190.3 %all-to-all-start.5 = ((bf16[32,2,65536]{2,1,0:T(2,128)(2,1)}), bf16[32,2,65536]{2,1,0:T(2,128)(2,1)}, u32[]{:S(2)}, u32[]{:S(2)}) async-start(bf16[32,2,65536]{2,1,0:T(2,128)(2,1)} %reshape.375), calls=%async_computation.5 | async-start | bytes 16777216 | tf_op jit(solution)/shard_map/all_to_all | solution.py:281
  1090.0 102.1 %copy-start.38 = (f32[5,48,16]{1,0,2:T(8,128)S(1)}, f32[5,48,16]{1,0,2:T(8,128)}, u32[]{:S(2)}) copy-start(f32[5,48,16]{1,0,2:T(8,128)} %copy-done.37) | copy-start | bytes 46084
  1090.0 102.2 %copy-start.24 = (f32[16,48,128]{2,1,0:T(8,128)S(1)}, f32[16,48,128]{2,1,0:T(8,128)}, u32[]{:S(2)}) copy-start(f32[16,48,128]{2,1,0:T(8,128)} %copy-done.23) | copy-start | bytes 1179652
  1184.5 191.0 %all-to-all-start.6 = ((bf16[32,2,65536]{2,1,0:T(2,128)(2,1)}), bf16[32,2,65536]{2,1,0:T(2,128)(2,1)}, u32[]{:S(2)}, u32[]{:S(2)}) async-start(bf16[32,2,65536]{2,1,0:T(2,128)(2,1)} %reshape.377), calls=%async_computation.6 | async-start | bytes 16777216 | tf_op jit(solution)/shard_map/all_to_all | solution.py:281
  1230.0 8.0 copy-start.14
  1286.9 14.1 copy-start.3
  1398.9 18.1 %copy-start.1 = (bf16[1,48,4,128]{3,2,1,0:T(4,128)(2,1)S(1)}, bf16[1,48,4,128]{3,2,1,0:T(4,128)(2,1)}, u32[]{:S(2)}) copy-start(bf16[1,48,4,128]{3,2,1,0:T(4,128)(2,1)} %param.13) | copy-start | bytes 147460
  (28 other events, 50.8 us)
Sparse Core Ops, SparseCore 0:
  11.0 56.5 all-gather.10
  70.6 55.4 all-gather.14
  129.0 75.4 all-gather.8
  207.2 69.0 all-gather.12
  279.1 75.6 all-gather.16
  357.6 75.7 all-gather.18

commit v2 on v1

--- a/solution.py
+++ b/solution.py
@@ -1,6 +1,10 @@
+import functools
+
 import jax
 import jax.numpy as jnp
 from jax import lax
+from jax.experimental import pallas as pl
+from jax.experimental.pallas import tpu as pltpu
 from jax.sharding import PartitionSpec as P
 
 D = 1024
@@ -11,6 +15,14 @@
 PATCHES = 128
 VEC_ROWS = 12
 
+PLANES = 4
+CORES = 2
+LANES = 128
+MESH_IDS = pl.DeviceIdType.MESH
+FIRST_GROUP = (0, 2, 4, 6)
+SECOND_GROUP = (1, 3, 5)
+VMEM_BYTES = 66 * 1000 * 1000
+
 
 norm_eps = 1e-05
 masked_score = -1e30
@@ -34,18 +46,405 @@
     return expo / jnp.sum(expo, -1, keepdims=True)
 
 
-def unpack(gathered):
-    return (
-        gathered[0].reshape(VARS, (PATCH_PIXELS + 1) * D),
-        gathered[1].reshape(D, 3 * D),
-        gathered[2].reshape(D, D),
-        gathered[3].reshape(D, 3 * D),
-        gathered[4].reshape(D, D),
-        gathered[5].reshape(D, FF),
-        gathered[6].reshape(FF, D),
-        gathered[7].reshape(VEC_ROWS, D),
-        gathered[8].reshape(PATCHES, D),
-    )
+class Place:
+    def __init__(self, wide, narrow):
+        self.columns = wide // (PLANES * CORES)
+        self.narrow = narrow
+        self.devices = wide * narrow
+        own = lax.axis_index("wide")
+        self.core = own % CORES
+        self.y = (own // CORES) % self.columns
+        self.z = own // (CORES * self.columns)
+        self.x = lax.axis_index("narrow")
+        near = 1 + self.z % 2
+        far = 3 * (1 - self.z // 2)
+        self.planes = (self.z, near, 6 - self.z - near - far, far)
+
+    def wide_of(self, z, y, core):
+        return (z * self.columns + y) * CORES + core
+
+    def block(self, z, y, x, core):
+        return self.wide_of(z, y, core) * self.narrow + x
+
+    def address(self, z, y, x, core):
+        return {"wide": self.wide_of(z, y, core), "narrow": x}
+
+    def other_y(self, step):
+        return (self.y + 1 + step) % self.columns
+
+    def other_x(self, step):
+        return (self.x + 1 + step) % self.narrow
+
+    def partners(self):
+        found = [self.address(z, self.y, self.x, self.core) for z in self.planes[1:]]
+        found += [self.address(self.z, self.other_y(i), self.x, self.core) for i in range(self.columns - 1)]
+        found += [self.address(self.z, self.y, self.other_x(i), self.core) for i in range(self.narrow - 1)]
+        found.append(self.address(self.z, self.y, self.x, 1 - self.core))
+        return found
+
+    def greet(self):
+        barrier = pltpu.get_barrier_semaphore()
+        found = self.partners()
+        for partner in found:
+            pl.semaphore_signal(barrier, inc=1, device_id=partner, device_id_type=MESH_IDS)
+        pl.semaphore_wait(barrier, len(found))
+
+
+def repeat(count, step):
+    if count <= 2:
+        for index in range(count):
+            step(index)
+    else:
+
+        def body(index, carry):
+            step(index)
+            return carry
+
+        lax.fori_loop(0, count, body, 0)
+
+
+def gather_kernel(wide, narrow, *refs):
+    kinds = (len(refs) - 3) // 2
+    shards, whole = refs[:kinds], refs[kinds : 2 * kinds]
+    send_sem, recv_sem, own_sem = refs[2 * kinds :]
+    here = Place(wide, narrow)
+    here.greet()
+
+    def push(kind, source, slot, target):
+        pltpu.make_async_remote_copy(
+            src_ref=source,
+            dst_ref=whole[kind].at[slot],
+            send_sem=send_sem.at[kind],
+            recv_sem=recv_sem.at[kind, slot],
+            device_id=target,
+            device_id_type=MESH_IDS,
+        ).start()
+
+    def arrived(kind, slot):
+        pltpu.make_async_copy(whole[kind].at[slot], whole[kind].at[slot], recv_sem.at[kind, slot]).wait()
+
+    def to_y(kind, source, slot):
+        repeat(
+            here.columns - 1,
+            lambda i: push(kind, source, slot, here.address(here.z, here.other_y(i), here.x, here.core)),
+        )
+
+    def to_x(kind, source, slot):
+        repeat(
+            here.narrow - 1,
+            lambda i: push(kind, source, slot, here.address(here.z, here.y, here.other_x(i), here.core)),
+        )
+
+    def to_sibling(kind, source, slot):
+        push(kind, source, slot, here.address(here.z, here.y, here.x, 1 - here.core))
+
+    own_slot = here.block(here.z, here.y, here.x, here.core)
+    groups = [(FIRST_GROUP, to_y, to_x), (SECOND_GROUP, to_x, to_y)]
+    for group, to_first, to_second in groups:
+        for kind in group:
+            pltpu.make_async_copy(shards[kind], whole[kind].at[own_slot], own_sem.at[kind]).start()
+            for z in here.planes[1:]:
+                push(kind, shards[kind], own_slot, here.address(z, here.y, here.x, here.core))
+            to_first(kind, shards[kind], own_slot)
+            to_second(kind, shards[kind], own_slot)
+            to_sibling(kind, shards[kind], own_slot)
+
+    def first_hop(z):
+        slot = here.block(z, here.y, here.x, here.core)
+        for group, to_first, to_second in groups:
+            for kind in group:
+                arrived(kind, slot)
+                source = whole[kind].at[slot]
+                to_first(kind, source, slot)
+                to_second(kind, source, slot)
+                to_sibling(kind, source, slot)
+
+    def second_hop(z):
+        def from_y(i):
+            slot = here.block(z, here.other_y(i), here.x, here.core)
+            for kind in FIRST_GROUP:
+                arrived(kind, slot)
+                to_x(kind, whole[kind].at[slot], slot)
+                to_sibling(kind, whole[kind].at[slot], slot)
+
+        def from_x(i):
+            slot = here.block(z, here.y, here.other_x(i), here.core)
+            for kind in SECOND_GROUP:
+                arrived(kind, slot)
+                to_y(kind, whole[kind].at[slot], slot)
+                to_sibling(kind, whole[kind].at[slot], slot)
+
+        repeat(here.columns - 1, from_y)
+        repeat(here.narrow - 1, from_x)
+
+    def third_hop(z):
+        def from_x(i):
+            x = here.other_x(i)
+
+            def from_column(y):
+                slot = here.block(z, y, x, here.core)
+                for kind in FIRST_GROUP:
+                    arrived(kind, slot)
+                    to_sibling(kind, whole[kind].at[slot], slot)
+
+            repeat(here.columns, lambda j: from_column((here.y + j) % here.columns))
+
+        def from_y(i):
+            y = here.other_y(i)
+
+            def from_row(x):
+                slot = here.block(z, y, x, here.core)
+                for kind in SECOND_GROUP:
+                    arrived(kind, slot)
+                    to_sibling(kind, whole[kind].at[slot], slot)
+
+            repeat(here.narrow, lambda j: from_row((here.x + j) % here.narrow))
+
+        repeat(here.narrow - 1, from_x)
+        repeat(here.columns - 1, from_y)
+
+    for step in range(PLANES + 2):
+        if 0 < step < PLANES:
+            first_hop(here.planes[step])
+        if 0 <= step - 1 < PLANES:
+            second_hop(here.planes[step - 1])
+        if 0 <= step - 2 < PLANES:
+            third_hop(here.planes[step - 2])
+
+    def from_sibling(index):
+        plane, rest = index // (here.columns * here.narrow), index % (here.columns * here.narrow)
+        slot = here.block(plane, rest // here.narrow, rest % here.narrow, 1 - here.core)
+        for kind in range(kinds):
+            arrived(kind, slot)
+
+    lax.fori_loop(0, here.devices // CORES, lambda i, c: (from_sibling(i), c)[1], 0)
+    for kind in range(kinds):
+        pltpu.make_async_copy(shards[kind], whole[kind].at[own_slot], own_sem.at[kind]).wait()
+        sent = whole[kind].at[pl.ds(0, here.devices - 1)]
+        pltpu.make_async_copy(sent, sent, send_sem.at[kind]).wait()
+
+
+def gather_all(shards, wide, narrow):
+    devices = wide * narrow
+    kinds = len(shards)
+    return pl.pallas_call(
+        functools.partial(gather_kernel, wide, narrow),
+        out_shape=[jax.ShapeDtypeStruct((devices,) + s.shape, s.dtype) for s in shards],
+        in_specs=[pl.BlockSpec(memory_space=pltpu.VMEM)] * kinds,
+        out_specs=[pl.BlockSpec(memory_space=pl.ANY)] * kinds,
+        scratch_shapes=[
+            pltpu.SemaphoreType.DMA((kinds,)),
+            pltpu.SemaphoreType.DMA((kinds, devices)),
+            pltpu.SemaphoreType.DMA((kinds,)),
+        ],
+        compiler_params=pltpu.CompilerParams(collective_id=0, has_side_effects=True),
+        name="gather_all",
+    )(*shards)
+
+
+def add_up(target, sources):
+    rows, cols = target.shape
+    high = min(rows, 16)
+    wide_step = min(cols, 1024)
+
+    def tile(index, carry):
+        here = pl.ds(pl.multiple_of(index * high, high), high)
+        for at in range(0, cols, wide_step):
+            there = pl.ds(at, wide_step)
+            total = sources[0][here, there].astype(jnp.float32)
+            for source in sources[1:]:
+                total = total + source[here, there].astype(jnp.float32)
+            target[here, there] = total.astype(target.dtype)
+        return carry
+
+    lax.fori_loop(0, rows // high, tile, 0)
+
+
+def scatter_kernel(wide, narrow, kinds, *refs):
+    terms, sums = refs[:kinds], refs[kinds : 2 * kinds]
+    own, near, second, first, planes = (refs[(2 + i) * kinds : (3 + i) * kinds] for i in range(5))
+    send_sem, own_sem, near_sem, second_sem, first_sem, plane_sem = refs[7 * kinds :]
+    here = Place(wide, narrow)
+    here.greet()
+    y_count, x_count = here.columns, here.narrow
+
+    def spot(z, y, x):
+        return (z * y_count + y) * x_count + x
+
+    def fetch(kind, z, y, x):
+        slot = spot(z, y, x)
+        pltpu.make_async_copy(
+            terms[kind].at[here.block(z, y, x, here.core)], own[kind].at[slot], own_sem.at[kind, slot]
+        ).start()
+        pltpu.make_async_remote_copy(
+            src_ref=terms[kind].at[here.block(z, y, x, 1 - here.core)],
+            dst_ref=near[kind].at[slot],
+            send_sem=send_sem.at[kind],
+            recv_sem=near_sem.at[kind, slot],
+            device_id=here.address(here.z, here.y, here.x, 1 - here.core),
+            device_id_type=MESH_IDS,
+        ).start()
+
+    def landed(buffer, kind, slot, sem):
+        pltpu.make_async_copy(buffer[kind].at[slot], buffer[kind].at[slot], sem.at[kind, slot]).wait()
+
+    def pair(kind, slot):
+        landed(own, kind, slot, own_sem)
+        landed(near, kind, slot, near_sem)
+        return [own[kind].at[slot], near[kind].at[slot]]
+
+    def send(kind, slot, buffer, place, sem, target):
+        pltpu.make_async_remote_copy(
+            src_ref=own[kind].at[slot],
+            dst_ref=buffer[kind].at[place],
+            send_sem=send_sem.at[kind],
+            recv_sem=sem.at[kind, place],
+            device_id=target,
+            device_id_type=MESH_IDS,
+        ).start()
+
+    def at(axis_first, a, b):
+        return (a, b) if axis_first == "y" else (b, a)
+
+    groups = []
+    for group, axis_first in ((FIRST_GROUP, "y"), (SECOND_GROUP, "x")):
+        if axis_first == "y":
+            a_own, b_own, a_count, b_count = here.y, here.x, y_count, x_count
+        else:
+            a_own, b_own, a_count, b_count = here.x, here.y, x_count, y_count
+        groups.append((group, axis_first, a_own, b_own, a_count, b_count))
+
+    def both(a_far, b_far, step):
+        for group, axis_first, a_own, b_own, a_count, b_count in groups:
+            a_steps = a_count - 1 if a_far else 1
+            b_steps = b_count - 1 if b_far else 1
+
+            def inner(i, j):
+                a_shift = 1 + i if a_far else 0
+                b_shift = 1 + j if b_far else 0
+                for kind in group:
+                    step(kind, axis_first, a_own, b_own, a_count, b_count, a_shift, b_shift)
+
+            repeat(a_steps, lambda i: repeat(b_steps, lambda j: inner(i, j)))
+
+    order = here.planes[::-1]
+
+    def start(z):
+        def step(kind, axis_first, a_own, b_own, a_count, b_count, a_shift, b_shift):
+            y, x = at(axis_first, (a_own + a_shift) % a_count, (b_own + b_shift) % b_count)
+            fetch(kind, z, y, x)
+
+        return step
+
+    def to_second(z):
+        def step(kind, axis_first, a_own, b_own, a_count, b_count, a_shift, b_shift):
+            a, b = (a_own + a_shift) % a_count, (b_own + b_shift) % b_count
+            y, x = at(axis_first, a, b)
+            slot = spot(z, y, x)
+            add_up(own[kind].at[slot], pair(kind, slot))
+            ty, tx = at(axis_first, a_own, b)
+            place = ((b_count - b_shift - 1) * PLANES + z) * a_count + a
+            send(kind, slot, second, place, second_sem, here.address(here.z, ty, tx, here.core))
+
+        return step
+
+    def from_second(kind, z, a, a_count, b_count):
+        found = []
+        for j in range(b_count - 1):
+            place = (j * PLANES + z) * a_count + a
+            landed(second, kind, place, second_sem)
+            found.append(second[kind].at[place])
+        return found
+
+    def to_first(z):
+        def step(kind, axis_first, a_own, b_own, a_count, b_count, a_shift, b_shift):
+            a = (a_own + a_shift) % a_count
+            y, x = at(axis_first, a, b_own)
+            slot = spot(z, y, x)
+            add_up(own[kind].at[slot], pair(kind, slot) + from_second(kind, z, a, a_count, b_count))
+            place = (a_count - a_shift - 1) * PLANES + z
+            send(kind, slot, first, place, first_sem, here.address(here.z, y, x, here.core))
+
+        return step
+
+    def collect(kind, z, a_own, a_count, b_count, slot):
+        found = pair(kind, slot) + from_second(kind, z, a_own, a_count, b_count)
+        for i in range(a_count - 1):
+            place = i * PLANES + z
+            landed(first, kind, place, first_sem)
+            found.append(first[kind].at[place])
+        return found
+
+    def to_plane(z):
+        def step(kind, axis_first, a_own, b_own, a_count, b_count, a_shift, b_shift):
+            slot = spot(z, here.y, here.x)
+            add_up(own[kind].at[slot], collect(kind, z, a_own, a_count, b_count, slot))
+            place = (here.z - z + PLANES) % PLANES - 1
+            send(kind, slot, planes, place, plane_sem, here.address(z, here.y, here.x, here.core))
+
+        return step
+
+    def finish(kind, axis_first, a_own, b_own, a_count, b_count, a_shift, b_shift):
+        slot = spot(here.z, here.y, here.x)
+        found = collect(kind, here.z, a_own, a_count, b_count, slot)
+        for place in range(PLANES - 1):
+            landed(planes, kind, place, plane_sem)
+            found.append(planes[kind].at[place])
+        add_up(sums[kind], found)
+
+    for z in order:
+        both(True, True, start(z))
+    for z in order:
+        both(False, True, start(z))
+        both(True, False, start(z))
+    for z in order:
+        both(False, False, start(z))
+    for z in order:
+        both(True, True, to_second(z))
+    for z in order:
+        both(False, True, to_second(z))
+        both(True, False, to_first(z))
+    for z in order[:-1]:
+        both(False, False, to_plane(z))
+    both(False, False, finish)
+    for kind in range(kinds):
+        sent = terms[kind].at[pl.ds(0, here.devices - 1)]
+        pltpu.make_async_copy(sent, sent, send_sem.at[kind]).wait()
+
+
+def scatter_all(terms, wide, narrow):
+    devices = wide * narrow
+    columns = wide // (PLANES * CORES)
+    kinds = len(terms)
+    shapes = [t.shape[1:] for t in terms]
+    half = devices // CORES
+    counts = []
+    for kind in range(kinds):
+        a_count, b_count = (columns, narrow) if kind in FIRST_GROUP else (narrow, columns)
+        counts.append((half, half, (b_count - 1) * PLANES * a_count, (a_count - 1) * PLANES, PLANES - 1))
+    scratch = [
+        pltpu.VMEM((counts[kind][stage],) + shapes[kind], terms[kind].dtype)
+        for stage in range(5)
+        for kind in range(kinds)
+    ]
+    scratch.append(pltpu.SemaphoreType.DMA((kinds,)))
+    scratch += [pltpu.SemaphoreType.DMA((kinds, max(c[stage] for c in counts))) for stage in range(5)]
+    return pl.pallas_call(
+        functools.partial(scatter_kernel, wide, narrow, kinds),
+        out_shape=[jax.ShapeDtypeStruct(s, jnp.float32) for s in shapes],
+        in_specs=[pl.BlockSpec(memory_space=pl.ANY)] * kinds,
+        out_specs=[pl.BlockSpec(memory_space=pltpu.VMEM)] * kinds,
+        scratch_shapes=scratch,
+        compiler_params=pltpu.CompilerParams(
+            collective_id=1, has_side_effects=True, vmem_limit_bytes=VMEM_BYTES
+        ),
+        name="scatter_all",
+    )(*terms)
+
+
+def small_size(shards):
+    need = sum(s.size for s in shards)
+    return -(-need // (16 * LANES)) * 16 * LANES
 
 
 def on_device(
@@ -63,28 +462,37 @@
     positions,
     cotangent,
 ):
-    gathered = (
-        lax.all_gather(embed_table, ("wide", "narrow"), axis=0, tiled=True),
-        lax.all_gather(agg_in, ("wide", "narrow"), axis=0, tiled=True),
-        lax.all_gather(agg_out, ("wide", "narrow"), axis=0, tiled=True),
-        lax.all_gather(attn_in, ("wide", "narrow"), axis=0, tiled=True),
-        lax.all_gather(attn_out, ("wide", "narrow"), axis=0, tiled=True),
-        lax.all_gather(mlp_in, ("wide", "narrow"), axis=0, tiled=True),
-        lax.all_gather(mlp_out, ("wide", "narrow"), axis=0, tiled=True),
-        lax.all_gather(vectors, ("wide", "narrow"), axis=0, tiled=True),
-        lax.all_gather(positions, ("wide", "narrow"), axis=0, tiled=True),
-    )
-    (
-        table_full,
-        agg_in_full,
-        agg_out_full,
-        attn_in_full,
-        attn_out_full,
-        mlp_in_full,
-        mlp_out_full,
-        vector_rows,
-        position_rows,
-    ) = unpack(gathered)
+    wide, narrow = lax.axis_size("wide"), lax.axis_size("narrow")
+    devices = wide * narrow
+    small = (embed_table, vectors, positions)
+    pad = small_size(small) - sum(s.size for s in small)
+    small_block = jnp.concatenate(small + (jnp.zeros((pad,), embed_table.dtype),)).reshape(-1, LANES)
+    gathered = gather_all(
+        (
+            mlp_in.reshape(-1, FF),
+            mlp_out.reshape(-1, D),
+            agg_in.reshape(-1, 3 * D),
+            attn_in.reshape(-1, 3 * D),
+            agg_out.reshape(-1, D),
+            attn_out.reshape(-1, D),
+            small_block,
+        ),
+        wide,
+        narrow,
+    )
+    mlp_in_full = gathered[0].reshape(D, FF)
+    mlp_out_full = gathered[1].reshape(FF, D)
+    agg_in_full = gathered[2].reshape(D, 3 * D)
+    attn_in_full = gathered[3].reshape(D, 3 * D)
+    agg_out_full = gathered[4].reshape(D, D)
+    attn_out_full = gathered[5].reshape(D, D)
+    small_rows = gathered[6].reshape(devices, -1)
+    cut_one = embed_table.size
+    cut_two = cut_one + vectors.size
+    cut_three = cut_two + positions.size
+    table_full = small_rows[:, :cut_one].reshape(VARS, (PATCH_PIXELS + 1) * D)
+    vector_rows = small_rows[:, cut_one:cut_two].reshape(VEC_ROWS, D)
+    position_rows = small_rows[:, cut_two:cut_three].reshape(PATCHES, D)
     head_size = D // HEADS
     score_scale = head_size ** (-0.5)
     length = PATCHES
@@ -271,32 +679,32 @@
         ],
         0,
     )
-    parts = (
-        grad_table, grad_agg_in, grad_agg_out, grad_attn_in, grad_attn_out,
-        grad_mlp_in, grad_mlp_out, grad_rows, grad_stream,
-    )
-    devices = lax.axis_size("wide") * lax.axis_size("narrow")
-    summed = tuple(
-        jnp.sum(
-            lax.all_to_all(
-                part.astype(bf16).reshape(devices, -1), ("wide", "narrow"), 0, 0, tiled=True
-            ).astype(single_float),
-            0,
-        )
-        for part in parts
-    )
+    small_terms = jnp.concatenate(
+        [
+            grad_table.astype(bf16).reshape(devices, -1),
+            grad_rows.astype(bf16).reshape(devices, -1),
+            grad_stream.astype(bf16).reshape(devices, -1),
+            jnp.zeros((devices, pad), bf16),
+        ],
+        1,
+    ).reshape(devices, -1, LANES)
+    large = (grad_mlp_in, grad_mlp_out, grad_agg_in, grad_attn_in, grad_agg_out, grad_attn_out)
+    summed = scatter_all(
+        tuple(g.astype(bf16).reshape(devices, -1, g.shape[1]) for g in large) + (small_terms,), wide, narrow
+    )
+    flat_small = summed[6].reshape(-1)
     return (
         result[None],
         fields_grad[None],
+        flat_small[:cut_one],
+        summed[2].reshape(-1),
+        summed[4].reshape(-1),
+        summed[3].reshape(-1),
+        summed[5].reshape(-1),
         summed[0].reshape(-1),
         summed[1].reshape(-1),
-        summed[2].reshape(-1),
-        summed[3].reshape(-1),
-        summed[4].reshape(-1),
-        summed[5].reshape(-1),
-        summed[6].reshape(-1),
-        summed[7].reshape(-1),
-        summed[8].reshape(-1),
+        flat_small[cut_one:cut_two],
+        flat_small[cut_two:cut_three],
     )
 
 

time: 1440 us -> 515 us (0.36)
  waiting for transfers between devices: 373 us -> 0 us
  Pallas kernels: 0 us -> 362 us
  local copies, waits for them, and re-layouts: 379 us -> 53.7 us
  other arithmetic: 320 us -> 19.2 us
  blocking collectives: 196 us -> 0 us
  starting transfers between devices: 56.7 us -> 0 us
    pallas_call x0 -> x2, Pallas kernels: none -> 362 us  [the longest x1 196 us: gather_all(): pl.pallas_call(functools.partial(gather_kernel, wide, narrow), out_shape=...]
    all_to_all x9 -> x0, waiting for transfers between devices: 225 us -> none  [on_device(): lax.all_to_all(part.astype(bf16).reshape(devices, -1), ('wide', 'narrow')...]
    all_gather x3 -> x0, blocking collectives: 196 us -> none  [the longest x1 74.1 us: on_device(): lax.all_gather(embed_table, ('wide', 'narrow'), axis=0, tiled=True)]
    all_to_all x7 -> x0, other arithmetic: 179 us -> none  [on_device(): lax.all_to_all(part.astype(bf16).reshape(devices, -1), ('wide', 'narrow')...]
    unnamed x112 -> x147, local copies, waits for them, and re-layouts: 179 us -> 17.3 us
    all_gather x6 -> x0, waiting for transfers between devices: 144 us -> none  [the longest x1 60.3 us: on_device(): lax.all_gather(mlp_out, ('wide', 'narrow'), axis=0, tiled=True)]
    all_to_all x8 -> x0, local copies, waits for them, and re-layouts: 96.5 us -> none  [on_device(): lax.all_to_all(part.astype(bf16).reshape(devices, -1), ('wide', 'narrow')...]
    reduce_sum x9 -> x0, other arithmetic: 80.3 us -> none  [on_device(): jnp.sum(lax.all_to_all(part.astype(bf16).reshape(devices, -1), ('wide', '...]
  transfers between devices with their start and end apart: 15 -> 0, of which waited for: 8 -> 0; matrix products, arithmetic and copies ran while one was open for 41% -> 0% of each run, Pallas kernels for 0% -> 0%
where the time goes in v2:
time: 515 us; the launch traced here: 511 us
  Pallas kernels  362 us (70%)
  matrix products  73.4 us (14%)
  local copies, waits for them, and re-layouts  53.7 us (10%)
  other arithmetic  19.2 us (4%)
    pallas_call x1, Pallas kernels, gather_all(): pl.pallas_call(functools.partial(gather_kernel, wide, narrow), out_shape=...  196 us
    pallas_call x1, Pallas kernels, scatter_all(): pl.pallas_call(functools.partial(scatter_kernel, wide, narrow, kinds), ou...  166 us
    unnamed x147, local copies, waits for them, and re-layouts  17.3 us

profile of v2, /device:TPU:8, one launch (start us, length us, event | category | flops | bytes accessed | tf_op | source)
XLA Modules:
  0.0 510.8 jit_solution(13060174979476807637)
XLA Ops:
  8.7 1.7 reshape.331.refs_2_
  10.4 1.7 reshape.332.refs_3_
  12.1 1.8 reshape.329.refs_0_
  14.7 196.4 %gather_all.1 = (bf16[32,32,4096]{2,1,0:T(8,128)(2,1)}, bf16[32,128,1024]{2,1,0:T(8,128)(2,1)}, bf16[32,32,3072]{2,1,0:T(8,128)(2,1)}, bf16[32,32,3072]{2,1,0:T(...) custom-call(bf16[32,4096]{1,0:T(8,128)(2,1)} %reshape.329.refs_0_, ...), custom_call_target="tpu_custom_call" | custom-call | tf_op jit(solution)/shard_map/gather_all/pallas_call | solution.py:230
  212.6 2.0 fusion.11
  217.0 3.4 fusion.3
  227.8 3.9 fusion.5
  234.8 5.3 %convolution_add_fusion = f32[128,4096]{1,0:T(8,128)S(1)} fusion(bf16[1024,4096]{1,0:T(8,128)(2,1)} %bitcast.194, f32[4096]{0:T(1024)S(1)} %bitcast.281, f32[128,1024]{1,0:T(8,128)S(1)} %get-tuple-element.117, f32[1024]{0:T(1024)S(1)} %bitcast.267, f32[1024]{0:T(1024)S(1)} %bitcast.258, f32[128]{0:T(128)S(1)} %fusion.50, f32[128]{0:T(128)S(1)} %broadcast_multiply_fusion.2), kind=kOutput, calls=%fused_computation.6 | convolution fusion | flops 1074921472 | bytes 11035648 | tf_op jit(solution)/shard_map/dot_general | solution.py:556
  240.2 2.1 fusion.23
  242.2 3.9 fusion.70
  246.2 3.7 multiply_reduce_fusion.5
  254.5 1.8 copy.99
  261.2 6.0 %multiply_reduce_fusion.6 = (bf16[1024]{0:T(1024)(128)(2,1)S(1)}, f32[128]{0:T(128)S(1)}, bf16[1024]{0:T(1024)(128)(2,1)S(1)}, f32[128,1024]{1,0:T(8,128)}) fusion(f32[128,1024]{1,0:T(8,128)S(1)} %copy-done.5, f32[128]{0:T(128)S(1)} %fusion.49, f32[128]{0:T(128)S(1)} %broadcast_multiply_fusion.3, f32[1024]{0:T(1024)S(1)} %bitcast.270, ...), kind=kOutput, calls=%fused_computation.78 | convolution fusion | flops 808712064 | bytes 8136192 | tf_op jit(solution)/shard_map/dot_general | solution.py:618
  271.8 1.8 copy.103
  273.7 2.8 convolution_convert_fusion.6
  276.5 2.0 copy.107
  279.7 1.8 reshape.370
  288.4 2.5 copy.104
  290.9 1.8 multiply_reduce_fusion.4
  292.7 3.5 fusion.9
  296.2 4.3 fusion.13
  300.7 2.2 copy.131
  302.9 2.7 reshape.364
  307.9 2.0 convolution_convert_fusion.5
  309.9 2.0 convolution_convert_fusion.4
  313.5 3.3 pad_maximum_fusion.refs_2_
  316.8 4.6 convolution_convert_fusion.2
  321.5 4.7 convolution_convert_fusion
  326.2 5.7 %convolution_convert_fusion.1 = bf16[1024,4096]{1,0:T(8,128)(2,1)} fusion(bf16[128,4096]{1,0:T(8,128)(2,1)S(1)} %copy-done.20, f32[128,1024]{1,0:T(8,128)S(1)} %copy-done.3, f32[1024]{0:T(1024)S(1)} %bitcast.268, f32[1024]{0:T(1024)S(1)} %bitcast.261, f32[128]{0:T(128)S(1)} %fusion.50, f32[128]{0:T(128)S(1)} %broadcast_multiply_fusion.2), kind=kOutput, calls=%fused_computation.2 | convolution fusion | flops 1078591488 | bytes 9970688 | tf_op jit(solution)/shard_map/dot_general | solution.py:573
  331.9 166.1 %scatter_all.1 = (f32[32,4096]{1,0:T(8,128)}, f32[128,1024]{1,0:T(8,128)}, f32[32,3072]{1,0:T(8,128)}, f32[32,3072]{1,0:T(8,128)}, f32[32,1024]{1,0:T(8,128)}, /*index=5*/f32[32,1024]{1,0:T(8,128)}, f32[96,128]{1,0:T(8,128)}) custom-call(bf16[32,32,4096]{2,1,0:T(8,128)(2,1)} %bitcast.198, bf16[32,128,1024]{2,1,0:T(8,128)(2,1)} %bitcast.193, ...), custom_call_target="tpu_custom_call" | custom-call | tf_op jit(solution)/shard_map/scatter_all/pallas_call | solution.py:432
  498.0 1.9 copy.119
  507.0 1.8 copy.121
  (242 shorter events, 57.8 us)
Async XLA Ops:
  0.7 13.2 %copy-start.50 = (bf16[131072]{0:T(1024)(128)(2,1)S(1)}, bf16[131072]{0:T(1024)(128)(2,1)}, u32[]{:S(2)}) copy-start(bf16[131072]{0:T(1024)(128)(2,1)} %param.22) | copy-start | bytes 786436
  8.7 216.2 %copy-start.24 = (f32[5,48,128]{2,1,0:T(8,128)}, f32[5,48,128]{2,1,0:T(8,128)S(1)}, u32[]{:S(2)}) copy-start(f32[5,48,128]{2,1,0:T(8,128)S(1)} %concatenate.30) | copy-start | bytes 368644
  227.5 5.6 %copy-start.4 = (f32[128,1024]{1,0:T(8,128)}, f32[128,1024]{1,0:T(8,128)S(1)}, u32[]{:S(2)}) copy-start(f32[128,1024]{1,0:T(8,128)S(1)} %get-tuple-element.113) | copy-start | bytes 1572868
  227.6 40.3 %copy-start.57 = (f32[128]{0:T(128)}, f32[128]{0:T(128)S(1)}, u32[]{:S(2)}) copy-start(f32[128]{0:T(128)S(1)} %broadcast_multiply_fusion.3) | copy-start | bytes 1540
  227.8 3.9 copy-start.62
  227.8 40.1 %copy-start.59 = (f32[128]{0:T(128)}, f32[128]{0:T(128)S(1)}, u32[]{:S(2)}) copy-start(f32[128]{0:T(128)S(1)} %fusion.49) | copy-start | bytes 1540
  234.0 6.1 %slice-start.2 = ((s8[8388608]{0:T(1024)(128)(4,1)}), s8[4194304]{0:T(1024)(128)(4,1)S(1)}, s32[]{:S(2)}) async-start(s8[8388608]{0:T(1024)(128)(4,1)} %bitcast.200), calls=%async_computation.2 | async-start | bytes 8388608
  234.5 11.6 %copy-start.2 = (f32[128,1024]{1,0:T(8,128)}, f32[128,1024]{1,0:T(8,128)S(1)}, u32[]{:S(2)}) copy-start(f32[128,1024]{1,0:T(8,128)S(1)} %get-tuple-element.117) | copy-start | bytes 1572868
  234.8 5.4 %slice-start.3 = ((s8[8388608]{0:T(1024)(128)(4,1)}), s8[4194304]{0:T(1024)(128)(4,1)S(1)}, s32[]{:S(2)}) async-start(s8[8388608]{0:T(1024)(128)(4,1)} %bitcast.200), calls=%async_computation.3 | async-start | bytes 8388608
  234.8 11.4 %slice-start = ((s8[8388608]{0:T(1024)(128)(4,1)}), s8[4194304]{0:T(1024)(128)(4,1)S(1)}, s32[]{:S(2)}) async-start(s8[8388608]{0:T(1024)(128)(4,1)} %bitcast.195), calls=%async_computation | async-start | bytes 8388608
  240.2 6.0 %slice-start.1 = ((s8[8388608]{0:T(1024)(128)(4,1)}), s8[4194304]{0:T(1024)(128)(4,1)S(1)}, s32[]{:S(2)}) async-start(s8[8388608]{0:T(1024)(128)(4,1)} %bitcast.195), calls=%async_computation.1 | async-start | bytes 8388608
  260.8 6.4 %copy-start.44 = (bf16[16,64,128]{2,1,0:T(8,128)(2,1)}, bf16[16,64,128]{2,1,0:T(8,128)(2,1)S(1)}, u32[]{:S(2)}) copy-start(bf16[16,64,128]{2,1,0:T(8,128)(2,1)S(1)} %fusion.21) | copy-start | bytes 786436
  261.1 6.0 %copy-start.46 = (bf16[16,64,128]{2,1,0:T(8,128)(2,1)}, bf16[16,64,128]{2,1,0:T(8,128)(2,1)S(1)}, u32[]{:S(2)}) copy-start(bf16[16,64,128]{2,1,0:T(8,128)(2,1)S(1)} %get-tuple-element.123) | copy-start | bytes 786436
  261.2 6.0 %copy-start.63 = (f32[128]{0:T(128)S(1)}, f32[128]{0:T(128)}, u32[]{:S(2)}) copy-start(f32[128]{0:T(128)} %copy-done.62) | copy-start | bytes 1540
  261.2 6.7 %copy-start.6 = (f32[128,1024]{1,0:T(8,128)S(1)}, f32[128,1024]{1,0:T(8,128)}, u32[]{:S(2)}) copy-start(f32[128,1024]{1,0:T(8,128)} %copy-done.4) | copy-start | bytes 1572868
  261.2 8.2 %copy-start.17 = (f32[128,1024]{1,0:T(8,128)S(1)}, f32[128,1024]{1,0:T(8,128)}, u32[]{:S(2)}) copy-start(f32[128,1024]{1,0:T(8,128)} %copy-done.16) | copy-start | bytes 1572868
  271.8 9.7 %copy-start.15 = (bf16[240,1024]{0,1:T(8,128)(2,1)S(1)}, bf16[240,1024]{0,1:T(8,128)(2,1)}, u32[]{:S(2)}) copy-start(bf16[240,1024]{0,1:T(8,128)(2,1)} %copy-done.14) | copy-start | bytes 1474564
  290.9 5.3 %copy-start.40 = (bf16[240,1024]{1,0:T(8,128)(2,1)S(1)}, bf16[240,1024]{1,0:T(8,128)(2,1)}, u32[]{:S(2)}) copy-start(bf16[240,1024]{1,0:T(8,128)(2,1)} %copy.107) | copy-start | bytes 1474564
  292.6 7.8 %copy-start.38 = (bf16[240,1024]{1,0:T(8,128)(2,1)}, bf16[240,1024]{1,0:T(8,128)(2,1)S(1)}, u32[]{:S(2)}) copy-start(bf16[240,1024]{1,0:T(8,128)(2,1)S(1)} %get-tuple-element.96) | copy-start | bytes 1474564
  296.1 4.3 copy-start.51
  296.1 4.3 copy-start.52
  296.2 4.3 copy-start.53
  296.2 4.3 copy-start.54
  296.2 4.3 copy-start.55
  296.2 4.3 copy-start.56
  302.9 5.0 copy-start.22
  302.9 5.0 copy-start.27
  321.5 4.7 copy-start.3
  321.5 4.7 copy-start.20
  498.0 10.9 %copy-start.49 = (f32[32,4096]{1,0:T(8,128)S(1)}, f32[32,4096]{1,0:T(8,128)}, u32[]{:S(2)}) copy-start(f32[32,4096]{1,0:T(8,128)} %get-tuple-element.37) | copy-start | bytes 1572868
  498.0 11.8 %copy-start.48 = (f32[128,1024]{1,0:T(8,128)S(1)}, f32[128,1024]{1,0:T(8,128)}, u32[]{:S(2)}) copy-start(f32[128,1024]{1,0:T(8,128)} %get-tuple-element.38) | copy-start | bytes 1572868
  498.0 12.6 %copy-start.1 = (bf16[1,48,4,128]{3,2,1,0:T(4,128)(2,1)S(1)}, bf16[1,48,4,128]{3,2,1,0:T(4,128)(2,1)}, u32[]{:S(2)}) copy-start(bf16[1,48,4,128]{3,2,1,0:T(4,128)(2,1)} %param.13) | copy-start | bytes 147460
  (36 other events, 78.9 us)

commit v3 on v1

--- a/solution.py
+++ b/solution.py
@@ -1,6 +1,10 @@
+import functools
+
 import jax
 import jax.numpy as jnp
 from jax import lax
+from jax.experimental import pallas as pl
+from jax.experimental.pallas import tpu as pltpu
 from jax.sharding import PartitionSpec as P
 
 D = 1024
@@ -11,6 +15,12 @@
 PATCHES = 128
 VEC_ROWS = 12
 
+PLANES = 4
+CORES = 2
+LANES = 128
+MESH_IDS = pl.DeviceIdType.MESH
+VMEM_BYTES = 66 * 1000 * 1000
+
 
 norm_eps = 1e-05
 masked_score = -1e30
@@ -34,18 +44,644 @@
     return expo / jnp.sum(expo, -1, keepdims=True)
 
 
-def unpack(gathered):
-    return (
-        gathered[0].reshape(VARS, (PATCH_PIXELS + 1) * D),
-        gathered[1].reshape(D, 3 * D),
-        gathered[2].reshape(D, D),
-        gathered[3].reshape(D, 3 * D),
-        gathered[4].reshape(D, D),
-        gathered[5].reshape(D, FF),
-        gathered[6].reshape(FF, D),
-        gathered[7].reshape(VEC_ROWS, D),
-        gathered[8].reshape(PATCHES, D),
-    )
+class Place:
+    def __init__(self, wide, narrow):
+        self.columns = wide // (PLANES * CORES)
+        self.narrow = narrow
+        self.devices = wide * narrow
+        own = lax.axis_index("wide")
+        self.core = own % CORES
+        self.y = (own // CORES) % self.columns
+        self.z = own // (CORES * self.columns)
+        self.x = lax.axis_index("narrow")
+        near = 1 + self.z % 2
+        far = 3 * (1 - self.z // 2)
+        self.planes = (self.z, near, 6 - self.z - near - far, far)
+
+    def wide_of(self, z, y, core):
+        return (z * self.columns + y) * CORES + core
+
+    def block(self, z, y, x, core):
+        return self.wide_of(z, y, core) * self.narrow + x
+
+    def address(self, z, y, x, core):
+        return {"wide": self.wide_of(z, y, core), "narrow": x}
+
+    def other_y(self, step):
+        return (self.y + 1 + step) % self.columns
+
+    def other_x(self, step):
+        return (self.x + 1 + step) % self.narrow
+
+    def partners(self):
+        found = [self.address(z, self.y, self.x, self.core) for z in self.planes[1:]]
+        found += [self.address(self.z, self.other_y(i), self.x, self.core) for i in range(self.columns - 1)]
+        found += [self.address(self.z, self.y, self.other_x(i), self.core) for i in range(self.narrow - 1)]
+        found.append(self.address(self.z, self.y, self.x, 1 - self.core))
+        return found
+
+    def greet(self):
+        barrier = pltpu.get_barrier_semaphore()
+        found = self.partners()
+        for partner in found:
+            pl.semaphore_signal(barrier, inc=1, device_id=partner, device_id_type=MESH_IDS)
+        pl.semaphore_wait(barrier, len(found))
+
+
+def repeat(count, step):
+    if count <= 2:
+        for index in range(count):
+            step(index)
+    else:
+
+        def body(index, carry):
+            step(index)
+            return carry
+
+        lax.fori_loop(0, count, body, 0)
+
+
+def lines_to_rows(lines, single, rows):
+    count, cols = rows.shape
+    each = cols // LANES
+    single[: lines.shape[0], :] = lines[...].astype(jnp.float32)
+    for at in range(each):
+        rows[:, at * LANES : (at + 1) * LANES] = single[pl.ds(at, count, stride=each), :].astype(rows.dtype)
+
+
+PHASES = (((6,1,0,1),(2,2,0,2)), ((4,2,0,2),(3,4,0,2)), ((3,4,2,4),(5,2,0,2)), ((0,4,0,2),), ((0,4,2,4),), ((1,4,0,2),), ((1,4,2,4),))
+
+
+COARSE_PHASES = (((6, 1, 0, 1), (2, 2, 0, 2)), ((4, 2, 0, 2), (3, 2, 0, 2)), ((5, 2, 0, 2), (0, 2, 0, 2)), ((1, 2, 0, 2),))
+MOST_PIECES = 2048
+
+
+def phase_parts(widths, devices, phases, coarse):
+    found = []
+    pieces_in_all = sum(last - first for phase in phases for _, _, first, last in phase)
+    for phase in phases if pieces_in_all * devices <= MOST_PIECES else coarse:
+        parts = []
+        for kind, pieces, first, last in phase:
+            width = widths[kind] // pieces
+            parts += [(kind, piece * width, width, piece % 2) for piece in range(first, last)]
+        found.append(parts)
+    return found
+
+
+def gather_kernel(widths, wide, narrow, *refs):
+    kinds = len(widths)
+    flats, whole, shards = (refs[i * kinds : (i + 1) * kinds] for i in range(3))
+    single, send_sem, recv_sem, own_sem = refs[3 * kinds :]
+    here = Place(wide, narrow)
+    for kind in range(kinds):
+        lines_to_rows(flats[kind], single, shards[kind])
+    here.greet()
+    own_slot = here.block(here.z, here.y, here.x, here.core)
+    for kind in range(kinds):
+        pltpu.make_async_copy(shards[kind], whole[kind].at[own_slot], own_sem.at[kind]).start()
+    phases, number = [], 0
+    for parts in phase_parts(widths, here.devices, PHASES, COARSE_PHASES):
+        phases.append([(number + i,) + part for i, part in enumerate(parts)])
+        number += len(parts)
+
+    def view(part, slot):
+        kind, at, width = part[1:4]
+        return whole[kind].at[slot, :, pl.ds(at, width)]
+
+    def push(part, slot, target, source=None):
+        pltpu.make_async_remote_copy(
+            src_ref=view(part, slot) if source is None else source,
+            dst_ref=view(part, slot),
+            send_sem=send_sem.at[part[1]],
+            recv_sem=recv_sem.at[part[0], slot],
+            device_id=target,
+            device_id_type=MESH_IDS,
+        ).start()
+
+    def arrived(part, slot):
+        pltpu.make_async_copy(view(part, slot), view(part, slot), recv_sem.at[part[0], slot]).wait()
+
+    def along(y_axis):
+        if y_axis:
+            return here.columns - 1, lambda i: here.address(here.z, here.other_y(i), here.x, here.core)
+        return here.narrow - 1, lambda i: here.address(here.z, here.y, here.other_x(i), here.core)
+
+    def to_axis(part, y_axis, slot, source=None):
+        count, address = along(y_axis)
+        repeat(count, lambda i: push(part, slot, address(i), source))
+
+    def to_sibling(part, slot, source=None):
+        push(part, slot, here.address(here.z, here.y, here.x, 1 - here.core), source)
+
+    across = (here.z + 2) % PLANES
+    beside = here.z + 1 - 2 * (here.z % 2)
+    beyond = (beside + 2) % PLANES
+
+    def send_own(parts):
+        for part in parts:
+            source = shards[part[1]].at[:, pl.ds(part[2], part[3])]
+            for y_axis in (part[4] == 0, part[4] != 0):
+                to_axis(part, y_axis, own_slot, source)
+            for z in (across, beside, beyond):
+                push(part, own_slot, here.address(z, here.y, here.x, here.core), source)
+            to_sibling(part, own_slot, source)
+
+    def first_hop(parts, z):
+        slot = here.block(z, here.y, here.x, here.core)
+        for part in parts:
+            arrived(part, slot)
+            for y_axis in (part[4] == 0, part[4] != 0):
+                to_axis(part, y_axis, slot)
+            to_sibling(part, slot)
+
+    def second_hop(parts, z, crosses):
+        for part in parts:
+            y_axis = part[4] == 0
+
+            def along_first(i):
+                slot = (
+                    here.block(z, here.other_y(i), here.x, here.core)
+                    if y_axis
+                    else here.block(z, here.y, here.other_x(i), here.core)
+                )
+                arrived(part, slot)
+                if crosses:
+                    to_axis(part, not y_axis, slot)
+                to_sibling(part, slot)
+
+            repeat(along(y_axis)[0], along_first)
+
+    def other_second_hop(parts, z):
+        for part in parts:
+            y_axis = part[4] != 0
+
+            def along_second(i):
+                slot = (
+                    here.block(z, here.other_y(i), here.x, here.core)
+                    if y_axis
+                    else here.block(z, here.y, here.other_x(i), here.core)
+                )
+                arrived(part, slot)
+                to_sibling(part, slot)
+
+            repeat(along(y_axis)[0], along_second)
+
+    def third_hop(parts, z, crosses):
+        for part in parts:
+
+            def one(i, j):
+                slot = here.block(z, here.other_y(i), here.other_x(j), here.core)
+                arrived(part, slot)
+                if crosses:
+                    push(part, slot, here.address(beside, here.y, here.x, here.core))
+                to_sibling(part, slot)
+
+            repeat(here.columns - 1, lambda i: repeat(here.narrow - 1, lambda j: one(i, j)))
+
+    def stage_b(parts):
+        second_hop(parts, here.z, True)
+        first_hop(parts, across)
+
+    def stage_c(parts):
+        third_hop(parts, here.z, True)
+        second_hop(parts, across, True)
+        first_hop(parts, beside)
+        other_second_hop(parts, here.z)
+
+    def stage_d(parts):
+        third_hop(parts, across, True)
+        first_hop(parts, beyond)
+        other_second_hop(parts, across)
+        second_hop(parts, beside, False)
+        other_second_hop(parts, beside)
+        third_hop(parts, beside, False)
+
+    def stage_e(parts):
+        second_hop(parts, beyond, False)
+        other_second_hop(parts, beyond)
+        third_hop(parts, beyond, False)
+
+    def stage_f(parts):
+        def from_sibling(index):
+            per_plane = here.columns * here.narrow
+            plane, rest = index // per_plane, index % per_plane
+            slot = here.block(plane, rest // here.narrow, rest % here.narrow, 1 - here.core)
+            for part in parts:
+                arrived(part, slot)
+
+        lax.fori_loop(0, here.devices // CORES, lambda i, c: (from_sibling(i), c)[1], 0)
+
+    stages = (send_own, stage_b, stage_c, stage_d, stage_e, stage_f)
+    for step in range(len(phases) + len(stages) - 1):
+        for lag, stage in enumerate(stages):
+            if 0 <= step - lag < len(phases):
+                stage(phases[step - lag])
+    for kind in range(kinds):
+        pltpu.make_async_copy(shards[kind], whole[kind].at[own_slot], own_sem.at[kind]).wait()
+        sent = whole[kind].at[pl.ds(0, here.devices - 1)]
+        pltpu.make_async_copy(sent, sent, send_sem.at[kind]).wait()
+
+
+def gather_all(flats, widths, wide, narrow):
+    devices = wide * narrow
+    kinds = len(flats)
+    shapes = [(flat.size // width, width) for flat, width in zip(flats, widths)]
+    lines = [flat.reshape(-1, LANES) for flat in flats]
+    parts = sum(len(phase) for phase in phase_parts(widths, devices, PHASES, COARSE_PHASES))
+    return pl.pallas_call(
+        functools.partial(gather_kernel, widths, wide, narrow),
+        out_shape=[jax.ShapeDtypeStruct((devices,) + s, f.dtype) for s, f in zip(shapes, flats)],
+        in_specs=[pl.BlockSpec(memory_space=pltpu.VMEM)] * kinds,
+        out_specs=[pl.BlockSpec(memory_space=pl.ANY)] * kinds,
+        scratch_shapes=[pltpu.VMEM(s, f.dtype) for s, f in zip(shapes, flats)]
+        + [
+            pltpu.VMEM((max(line.shape[0] for line in lines), LANES), jnp.float32),
+            pltpu.SemaphoreType.DMA((kinds,)),
+            pltpu.SemaphoreType.DMA((parts, devices)),
+            pltpu.SemaphoreType.DMA((kinds,)),
+        ],
+        compiler_params=pltpu.CompilerParams(collective_id=0, has_side_effects=True),
+        name="gather_all",
+    )(*lines)
+
+
+def add_up(target, sources):
+    rows, cols = target.shape
+    high = min(rows, 16)
+    wide_step = next(w for w in (1024, 768, 512, 256, LANES) if cols % w == 0)
+
+    def tile(index, carry):
+        here = pl.ds(pl.multiple_of(index * high, high), high)
+        for at in range(0, cols, wide_step):
+            there = pl.ds(at, wide_step)
+            total = sources[0][here, there].astype(jnp.float32)
+            for source in sources[1:]:
+                total = total + source[here, there].astype(jnp.float32)
+            target[here, there] = total.astype(target.dtype)
+        return carry
+
+    lax.fori_loop(0, rows // high, tile, 0)
+
+
+def add_up_lines(lines, shape, first, sources):
+    rows, cols = shape
+    width = sources[0].shape[1]
+    high = min(rows, 16)
+    each = cols // LANES
+
+    def tile(index, carry):
+        here = pl.ds(pl.multiple_of(index * high, high), high)
+        for at in range(width // LANES):
+            there = pl.ds(at * LANES, LANES)
+            total = sources[0][here, there].astype(jnp.float32)
+            for source in sources[1:]:
+                total = total + source[here, there].astype(jnp.float32)
+            lines[pl.ds(index * (high * each) + first // LANES + at, high, stride=each), :] = total
+        return carry
+
+    lax.fori_loop(0, rows // high, tile, 0)
+
+
+SUM_PHASES = (
+    ((1, 4, 0, 2),),
+    ((1, 4, 2, 4),),
+    ((0, 4, 0, 2),),
+    ((0, 4, 2, 4),),
+    ((5, 2, 0, 2), (3, 4, 0, 2)),
+    ((3, 4, 2, 4), (4, 2, 0, 2), (6, 1, 0, 1)),
+    ((2, 4, 0, 2),),
+    ((2, 4, 2, 4),),
+)
+COARSE_SUM_PHASES = (((1, 2, 0, 2),), ((0, 2, 0, 2),), ((5, 2, 0, 2), (3, 2, 0, 2), (4, 2, 0, 2)), ((2, 2, 0, 2), (6, 1, 0, 1)))
+SHARED = 2
+TILE = 256
+
+
+def scatter_kernel(direct, shapes, wide, narrow, *refs):
+    kinds = len(shapes)
+    refs = list(refs)
+
+    def take(count):
+        found = refs[:count]
+        del refs[:count]
+        return found
+
+    inputs = [take(2) if direct[kind] else take(1) for kind in range(kinds)]
+    sums = take(kinds)
+    own, second, first, planes, cross = (take(kinds) for _ in range(5))
+    local = [take(3) if direct[kind] and kind == SHARED else take(2) if direct[kind] else take(1) for kind in range(kinds)]
+    send_sem, near_send_sem, own_sem, near_sem, second_sem, first_sem, plane_sem, cross_sem = refs
+    here = Place(wide, narrow)
+    here.greet()
+    y_count, x_count = here.columns, here.narrow
+    half = here.devices // CORES
+    sibling = here.address(here.z, here.y, here.x, 1 - here.core)
+    across = (here.z + 2) % PLANES
+    beside = here.z + 1 - 2 * (here.z % 2)
+    phases, number = [], 0
+    for parts in phase_parts([s[1] for s in shapes], here.devices, SUM_PHASES, COARSE_SUM_PHASES):
+        phases.append([(number + i,) + part for i, part in enumerate(parts)])
+        number += len(parts)
+
+    def spot(z, y, x):
+        return (z * y_count + y) * x_count + x
+
+    def mine(kind):
+        if not direct[kind]:
+            pairs = [(inputs[kind][0].at[here.core], own[kind])]
+        else:
+            left, right = inputs[kind]
+            low = pl.ds(0, right.shape[0])
+            if kind == SHARED:
+                pairs = [(left.at[:, here.core], local[kind][0]), (right, local[kind][1])]
+            else:
+                pairs = [(left.at[:, here.core], local[kind][0].at[:, :, low]), (right, local[kind][1].at[low])]
+        return [pltpu.make_async_copy(source, target, own_sem.at[kind, i]) for i, (source, target) in enumerate(pairs)]
+
+    def theirs(kind):
+        if not direct[kind]:
+            pairs = [(inputs[kind][0].at[1 - here.core], local[kind][0])]
+        else:
+            left, right = inputs[kind]
+            high = pl.ds(right.shape[0], right.shape[0])
+            if kind == SHARED:
+                pairs = [(right, local[kind][2])]
+            else:
+                pairs = [(left.at[:, 1 - here.core], local[kind][0].at[:, :, high]), (right, local[kind][1].at[high])]
+        return [
+            pltpu.make_async_remote_copy(
+                src_ref=source,
+                dst_ref=target,
+                send_sem=near_send_sem.at[kind, i],
+                recv_sem=near_sem.at[kind, i],
+                device_id=sibling,
+                device_id_type=MESH_IDS,
+            )
+            for i, (source, target) in enumerate(pairs)
+        ]
+
+    def fetch(kind):
+        for copy in mine(kind) + theirs(kind):
+            copy.start()
+
+    def fetched(kind):
+        for copy in mine(kind):
+            copy.wait()
+        for copy in theirs(kind):
+            copy.wait_recv()
+        if direct[kind] and kind == SHARED:
+            add_up(local[kind][1], [local[kind][1], local[kind][2]])
+
+    def multiply(part):
+        _, kind, at, width, _ = part
+        if not direct[kind]:
+            return
+        left, right = local[kind][:2]
+        groups, rows, depth = left.shape
+        take_groups = min(groups, max(1, 512 // rows))
+        block_rows = shapes[kind][0]
+        slots = take_groups * rows // block_rows
+        steps = groups // take_groups
+
+        def one(index, carry):
+            column = pl.multiple_of(at + (index // steps) * TILE, TILE)
+            group = index % steps
+            factor = left[pl.ds(group * take_groups, take_groups), :, :].reshape(take_groups * rows, depth)
+            block = jnp.dot(factor, right[:, pl.ds(column, TILE)], preferred_element_type=jnp.float32)
+            own[kind][pl.ds(group * slots, slots), :, pl.ds(column, TILE)] = block.astype(jnp.bfloat16).reshape(
+                slots, block_rows, TILE
+            )
+            return carry
+
+        lax.fori_loop(0, steps * (width // TILE), one, 0)
+
+    def view(buffer, part, place):
+        return buffer[part[1]].at[place, :, pl.ds(part[2], part[3])]
+
+    def landed(buffer, part, place, sem):
+        pltpu.make_async_copy(view(buffer, part, place), view(buffer, part, place), sem.at[part[0], place]).wait()
+        return view(buffer, part, place)
+
+    def terms_of(part, slot):
+        found = [view(own, part, slot)]
+        if not direct[part[1]]:
+            found.append(view(local_near, part, slot))
+        return found
+
+    local_near = [refs_of[0] for refs_of in local]
+
+    def send(part, slot, buffer, place, sem, target):
+        pltpu.make_async_remote_copy(
+            src_ref=view(own, part, slot),
+            dst_ref=view(buffer, part, place),
+            send_sem=send_sem.at[part[1]],
+            recv_sem=sem.at[part[0], place],
+            device_id=target,
+            device_id_type=MESH_IDS,
+        ).start()
+
+    def settle(part, slot, found):
+        if len(found) > 1:
+            add_up(found[0], found)
+
+    def axes(part):
+        if part[4] == 0:
+            return here.y, here.x, y_count, x_count
+        return here.x, here.y, x_count, y_count
+
+    def place_of(part, a, b):
+        return (a, b) if part[4] == 0 else (b, a)
+
+    def cross_place(part, z, a_shift, b_shift, a_count, b_count):
+        return ((z // 2) * (a_count - 1) + a_shift - 1) * (b_count - 1) + b_shift - 1
+
+    def far_pairs(part, step):
+        a_own, b_own, a_count, b_count = axes(part)
+        repeat(a_count - 1, lambda i: repeat(b_count - 1, lambda j: step(1 + i, 1 + j)))
+
+    def loop(count, step):
+        lax.fori_loop(0, count, lambda i, carry: (step(i), carry)[1], 0)
+
+    def plane_in_order(i):
+        base = beside + (i // 2) * (here.z - beside)
+        return (base + 2 * (1 - i % 2)) % PLANES
+
+    def to_beside(part):
+        a_own, b_own, a_count, b_count = axes(part)
+
+        def one(z, a_shift, b_shift):
+            y, x = place_of(part, (a_own + a_shift) % a_count, (b_own + b_shift) % b_count)
+            slot = spot(z, y, x)
+            settle(part, slot, terms_of(part, slot))
+            place = cross_place(part, z, a_shift, b_shift, a_count, b_count)
+            send(part, slot, cross, place, cross_sem, here.address(beside, here.y, here.x, here.core))
+
+        loop(2, lambda i: far_pairs(part, lambda p, q: one(plane_in_order(i), p, q)))
+
+    def to_second(part, z, a_shift, b_shift, crosses):
+        a_own, b_own, a_count, b_count = axes(part)
+        a, b = (a_own + a_shift) % a_count, (b_own + b_shift) % b_count
+        y, x = place_of(part, a, b)
+        slot = spot(z, y, x)
+        found = terms_of(part, slot)
+        if crosses:
+            found.append(
+                landed(cross, part, cross_place(part, z, a_shift, b_shift, a_count, b_count), cross_sem)
+            )
+        settle(part, slot, found)
+        ty, tx = place_of(part, a_own, b)
+        place = ((b_count - b_shift - 1) * PLANES + z) * a_count + a
+        send(part, slot, second, place, second_sem, here.address(here.z, ty, tx, here.core))
+
+    def from_second(part, z, a):
+        _, _, a_count, b_count = axes(part)
+        return [
+            landed(second, part, (j * PLANES + z) * a_count + a, second_sem) for j in range(b_count - 1)
+        ]
+
+    def to_first(part, z, a_shift, crosses):
+        a_own, b_own, a_count, b_count = axes(part)
+        a = (a_own + a_shift) % a_count
+        y, x = place_of(part, a, b_own)
+        slot = spot(z, y, x)
+        found = terms_of(part, slot)
+        if crosses:
+            found += from_second(part, z, a)
+        settle(part, slot, found)
+        place = (a_count - a_shift - 1) * PLANES + z
+        send(part, slot, first, place, first_sem, here.address(here.z, y, x, here.core))
+
+    def collect(part, z):
+        a_own, b_own, a_count, b_count = axes(part)
+        found = terms_of(part, spot(z, here.y, here.x)) + from_second(part, z, a_own)
+        return found + [landed(first, part, i * PLANES + z, first_sem) for i in range(a_count - 1)]
+
+    def to_plane(part, z):
+        slot = spot(z, here.y, here.x)
+        settle(part, slot, collect(part, z))
+        place = (here.z - z + PLANES) % PLANES - 1
+        send(part, slot, planes, place, plane_sem, here.address(z, here.y, here.x, here.core))
+
+    seen = set()
+
+    def stage_fetch(parts):
+        for part in parts:
+            if part[1] not in seen:
+                fetch(part[1])
+            seen.add(part[1])
+
+    ready = set()
+
+    def stage_terms(parts):
+        for part in parts:
+            if part[1] not in ready:
+                fetched(part[1])
+            ready.add(part[1])
+            multiply(part)
+            to_beside(part)
+
+    def stage_out(parts):
+        for part in parts:
+            b_count = axes(part)[3]
+            a_count = axes(part)[2]
+            loop(
+                4,
+                lambda i: repeat(b_count - 1, lambda j: to_second(part, plane_in_order(i), 0, 1 + j, False)),
+            )
+            loop(2, lambda i: repeat(a_count - 1, lambda j: to_first(part, plane_in_order(i), 1 + j, False)))
+            loop(2, lambda i: far_pairs(part, lambda p, q: to_second(part, plane_in_order(2 + i), p, q, True)))
+
+    def stage_first(parts):
+        for part in parts:
+            a_count = axes(part)[2]
+            loop(2, lambda i: repeat(a_count - 1, lambda j: to_first(part, plane_in_order(2 + i), 1 + j, True)))
+
+    def stage_planes(parts):
+        for part in parts:
+            loop(3, lambda i: to_plane(part, plane_in_order((2 + i) % 3)))
+
+    def stage_finish(parts):
+        for part in parts:
+            found = collect(part, here.z)
+            found += [landed(planes, part, place, plane_sem) for place in range(PLANES - 1)]
+            add_up_lines(sums[part[1]], shapes[part[1]], part[2], found)
+
+    stages = (stage_fetch, stage_terms, stage_out, stage_first, stage_planes, stage_finish)
+    for step in range(len(phases) + len(stages) - 1):
+        for lag, stage in enumerate(stages):
+            if 0 <= step - lag < len(phases):
+                stage(phases[step - lag])
+    for kind in range(kinds):
+        for copy in theirs(kind):
+            copy.wait_send()
+        sent = own[kind].at[pl.ds(0, half - 1)]
+        pltpu.make_async_copy(sent, sent, send_sem.at[kind]).wait()
+
+
+def scatter_all(factors, shapes, wide, narrow):
+    devices = wide * narrow
+    columns = wide // (PLANES * CORES)
+    kinds = len(shapes)
+    half = devices // CORES
+    low = jnp.bfloat16
+    direct, operands, scratch = [], [], []
+    for kind, given in enumerate(factors):
+        rows, cols = shapes[kind]
+        direct.append(len(given) == 2 and rows % 16 == 0)
+        if direct[kind]:
+            left, right = given
+            operands += [left.reshape(PLANES * columns, CORES, narrow * rows, left.shape[1]), right]
+        else:
+            terms = given[0]
+            if len(given) == 2:
+                terms = jnp.dot(given[0], given[1], preferred_element_type=jnp.float32).astype(low)
+            terms = terms.reshape(PLANES * columns, CORES, narrow, rows, cols)
+            operands.append(jnp.moveaxis(terms, 1, 0).reshape(CORES, half, rows, cols))
+    orders = ((columns, narrow), (narrow, columns))
+    counts = (
+        half,
+        max((b - 1) * PLANES * a for a, b in orders),
+        max((a - 1) * PLANES for a, b in orders),
+        PLANES - 1,
+        2 * (columns - 1) * (narrow - 1),
+    )
+    for stage in range(5):
+        for kind in range(kinds):
+            if stage == 0 and not direct[kind]:
+                scratch.append(pltpu.VMEM((half,) + shapes[kind], low))
+            else:
+                scratch.append(pltpu.VMEM((counts[stage],) + shapes[kind], low))
+    for kind in range(kinds):
+        rows, cols = shapes[kind]
+        if not direct[kind]:
+            scratch.append(pltpu.VMEM((half, rows, cols), low))
+            continue
+        tokens = factors[kind][1].shape[0]
+        depth = tokens if kind == SHARED else 2 * tokens
+        scratch.append(pltpu.VMEM((PLANES * columns, narrow * rows, depth), low))
+        scratch.append(pltpu.VMEM((depth, cols), low))
+        if kind == SHARED:
+            scratch.append(pltpu.VMEM((depth, cols), low))
+    widths = [s[1] for s in shapes]
+    parts = sum(len(phase) for phase in phase_parts(widths, devices, SUM_PHASES, COARSE_SUM_PHASES))
+    scratch += [pltpu.SemaphoreType.DMA((kinds,))] + [pltpu.SemaphoreType.DMA((kinds, 2))] * 3
+    scratch += [pltpu.SemaphoreType.DMA((parts, counts[stage])) for stage in range(1, 5)]
+    return pl.pallas_call(
+        functools.partial(scatter_kernel, tuple(direct), tuple(shapes), wide, narrow),
+        out_shape=[jax.ShapeDtypeStruct((s[0] * s[1] // LANES, LANES), jnp.float32) for s in shapes],
+        in_specs=[pl.BlockSpec(memory_space=pl.ANY)] * len(operands),
+        out_specs=[pl.BlockSpec(memory_space=pltpu.VMEM)] * kinds,
+        scratch_shapes=scratch,
+        compiler_params=pltpu.CompilerParams(
+            collective_id=1, has_side_effects=True, vmem_limit_bytes=VMEM_BYTES
+        ),
+        name="scatter_all",
+    )(*operands)
+
+
+def small_size(shards):
+    need = sum(s.size for s in shards)
+    return -(-need // (16 * LANES)) * 16 * LANES
 
 
 def on_device(
@@ -63,28 +699,38 @@
     positions,
     cotangent,
 ):
-    gathered = (
-        lax.all_gather(embed_table, ("wide", "narrow"), axis=0, tiled=True),
-        lax.all_gather(agg_in, ("wide", "narrow"), axis=0, tiled=True),
-        lax.all_gather(agg_out, ("wide", "narrow"), axis=0, tiled=True),
-        lax.all_gather(attn_in, ("wide", "narrow"), axis=0, tiled=True),
-        lax.all_gather(attn_out, ("wide", "narrow"), axis=0, tiled=True),
-        lax.all_gather(mlp_in, ("wide", "narrow"), axis=0, tiled=True),
-        lax.all_gather(mlp_out, ("wide", "narrow"), axis=0, tiled=True),
-        lax.all_gather(vectors, ("wide", "narrow"), axis=0, tiled=True),
-        lax.all_gather(positions, ("wide", "narrow"), axis=0, tiled=True),
-    )
-    (
-        table_full,
-        agg_in_full,
-        agg_out_full,
-        attn_in_full,
-        attn_out_full,
-        mlp_in_full,
-        mlp_out_full,
-        vector_rows,
-        position_rows,
-    ) = unpack(gathered)
+    wide, narrow = lax.axis_size("wide"), lax.axis_size("narrow")
+    devices = wide * narrow
+    small = (embed_table, vectors, positions)
+    pad = small_size(small) - sum(s.size for s in small)
+    small_block = jnp.concatenate(small + (jnp.zeros((pad,), embed_table.dtype),))
+    gathered = gather_all(
+        (
+            mlp_in,
+            mlp_out,
+            agg_in,
+            attn_in,
+            agg_out,
+            attn_out,
+            small_block,
+        ),
+        (FF, D, 3 * D, 3 * D, D, D, LANES),
+        wide,
+        narrow,
+    )
+    mlp_in_full = gathered[0].reshape(D, FF)
+    mlp_out_full = gathered[1].reshape(FF, D)
+    agg_in_full = gathered[2].reshape(D, 3 * D)
+    attn_in_full = gathered[3].reshape(D, 3 * D)
+    agg_out_full = gathered[4].reshape(D, D)
+    attn_out_full = gathered[5].reshape(D, D)
+    small_rows = gathered[6].reshape(devices, -1)
+    cut_one = embed_table.size
+    cut_two = cut_one + vectors.size
+    cut_three = cut_two + positions.size
+    table_full = small_rows[:, :cut_one].reshape(VARS, (PATCH_PIXELS + 1) * D)
+    vector_rows = small_rows[:, cut_one:cut_two].reshape(VEC_ROWS, D)
+    position_rows = small_rows[:, cut_two:cut_three].reshape(PATCHES, D)
     head_size = D // HEADS
     score_scale = head_size ** (-0.5)
     length = PATCHES
@@ -157,19 +803,16 @@
     grad_output = cotangent[0].astype(single_float)
     grad_branch2 = grad_output.astype(bf16)
     grad_fc2_bias = jnp.sum(grad_branch2.astype(single_float), 0)
-    grad_mlp_out = jnp.dot(activated.T, grad_branch2, preferred_element_type=single_float)
     grad_activated = jnp.dot(grad_branch2, mlp_out_full.T, preferred_element_type=single_float)
     gelu_value, gelu_pull = jax.vjp(gelu_exact, hidden)
     grad_hidden = gelu_pull(grad_activated)[0].astype(bf16)
     grad_fc1_bias = jnp.sum(grad_hidden.astype(single_float), 0)
-    grad_mlp_in = jnp.dot(normed2.T, grad_hidden, preferred_element_type=single_float)
     grad_normed2 = jnp.dot(grad_hidden, mlp_in_full.T, preferred_element_type=single_float)
     norm_value2, norm2_pull = jax.vjp(layer_norm, stream1, row_values[5], row_values[6])
     back_stream1, grad_gain2, grad_shift2 = norm2_pull(grad_normed2)
     grad_stream1 = grad_output + back_stream1
     grad_branch1 = grad_stream1.astype(bf16)
     grad_proj_bias = jnp.sum(grad_branch1.astype(single_float), 0)
-    grad_attn_out = jnp.dot(attended.T, grad_branch1, preferred_element_type=single_float)
     grad_attended = (
         jnp.dot(grad_branch1, attn_out_full.T, preferred_element_type=single_float)
         .astype(bf16)
@@ -206,13 +849,11 @@
         1,
     ).astype(bf16)
     grad_query_bias = jnp.sum(grad_projected[:, :D].astype(single_float), 0)
-    grad_attn_in = jnp.dot(normed1.T, grad_projected, preferred_element_type=single_float)
     grad_normed1 = jnp.dot(grad_projected, attn_in_full.T, preferred_element_type=single_float)
     norm_value1, norm1_pull = jax.vjp(layer_norm, stream, row_values[1], row_values[2])
     back_stream, grad_gain1, grad_shift1 = norm1_pull(grad_normed1)
     grad_stream = grad_stream1 + back_stream
     grad_agg_branch = grad_stream.astype(bf16)
-    grad_agg_out = jnp.dot(mixture.T, grad_agg_branch, preferred_element_type=single_float)
     grad_mixture = (
         jnp.dot(grad_agg_branch, agg_out_full.T, preferred_element_type=single_float)
         .astype(bf16)
@@ -242,17 +883,24 @@
     dots_wide = jnp.repeat(grad_dots, head_size, 1)
     grad_agg_query = jnp.sum(dots_wide * table_keys, 0)
     grad_table_kv = jnp.concatenate([dots_wide * query_wide, grad_table_values], 1).astype(bf16)
-    grad_agg_kv = jnp.dot(table_rows.T, grad_table_kv, preferred_element_type=single_float)
     grad_table = (
         jnp.dot(grad_table_kv, agg_in_full[:, D:].T, preferred_element_type=single_float)
         .reshape(PATCH_PIXELS + 1, VARS, D)
         .transpose(1, 0, 2)
     )
-    grad_agg_qproj = query_row.astype(single_float)[:, None] * grad_agg_query[None, :]
+    filling = 2 * LANES - table_rows.shape[0] - 1
+    table_and_query = jnp.concatenate([table_rows, query_row[None, :], jnp.zeros((filling, D), bf16)], 0)
+    grad_table_and_query = jnp.concatenate(
+        [
+            jnp.pad(grad_table_kv, ((0, 0), (D, 0))),
+            jnp.pad(grad_agg_query.astype(bf16)[None, :], ((0, 0), (0, 2 * D))),
+            jnp.zeros((filling, 3 * D), bf16),
+        ],
+        0,
+    )
     grad_query_row = jnp.dot(
         agg_in_full[:, :D].astype(single_float), grad_agg_query, precision=highest_precision
     )
-    grad_agg_in = jnp.concatenate([grad_agg_qproj, grad_agg_kv], 1)
     grad_rows = jnp.concatenate(
         [
             jnp.stack(
@@ -271,32 +919,54 @@
         ],
         0,
     )
-    parts = (
-        grad_table, grad_agg_in, grad_agg_out, grad_attn_in, grad_attn_out,
-        grad_mlp_in, grad_mlp_out, grad_rows, grad_stream,
-    )
-    devices = lax.axis_size("wide") * lax.axis_size("narrow")
-    summed = tuple(
-        jnp.sum(
-            lax.all_to_all(
-                part.astype(bf16).reshape(devices, -1), ("wide", "narrow"), 0, 0, tiled=True
-            ).astype(single_float),
-            0,
+    small_terms = jnp.concatenate(
+        [
+            grad_table.astype(bf16).reshape(devices, -1),
+            grad_rows.astype(bf16).reshape(devices, -1),
+            grad_stream.astype(bf16).reshape(devices, -1),
+            jnp.zeros((devices, pad), bf16),
+        ],
+        1,
+    ).reshape(devices, -1, LANES)
+    shapes = tuple(
+        (count // (cols * devices), cols)
+        for count, cols in (
+            (D * FF, FF),
+            (FF * D, D),
+            (3 * D * D, 3 * D),
+            (3 * D * D, 3 * D),
+            (D * D, D),
+            (D * D, D),
+            (small_terms.size, LANES),
         )
-        for part in parts
-    )
+    )
+    summed = scatter_all(
+        (
+            (normed2.T, grad_hidden),
+            (activated.T, grad_branch2),
+            (table_and_query.T, grad_table_and_query),
+            (normed1.T, grad_projected),
+            (mixture.T, grad_agg_branch),
+            (attended.T, grad_branch1),
+            (small_terms,),
+        ),
+        shapes,
+        wide,
+        narrow,
+    )
+    flat_small = summed[6].reshape(-1)
     return (
         result[None],
         fields_grad[None],
+        flat_small[:cut_one],
+        summed[2].reshape(-1),
+        summed[4].reshape(-1),
+        summed[3].reshape(-1),
+        summed[5].reshape(-1),
         summed[0].reshape(-1),
         summed[1].reshape(-1),
-        summed[2].reshape(-1),
-        summed[3].reshape(-1),
-        summed[4].reshape(-1),
-        summed[5].reshape(-1),
-        summed[6].reshape(-1),
-        summed[7].reshape(-1),
-        summed[8].reshape(-1),
+        flat_small[cut_one:cut_two],
+        flat_small[cut_two:cut_three],
     )
 
 

time: 1440 us -> 411 us (0.29)
  waiting for transfers between devices: 373 us -> 0 us
  local copies, waits for them, and re-layouts: 379 us -> 38.9 us
  other arithmetic: 320 us -> 17.7 us
  Pallas kernels: 0 us -> 298 us
  blocking collectives: 196 us -> 0 us
  starting transfers between devices: 56.7 us -> 0 us
  matrix products: 84.9 us -> 47 us
    pallas_call x0 -> x2, Pallas kernels: none -> 298 us  [the longest x1 153 us: scatter_all(): pl.pallas_call(functools.partial(scatter_kernel, tuple(direct), tuple(sha...]
    all_to_all x9 -> x0, waiting for transfers between devices: 225 us -> none  [on_device(): lax.all_to_all(part.astype(bf16).reshape(devices, -1), ('wide', 'narrow')...]
    all_gather x3 -> x0, blocking collectives: 196 us -> none  [the longest x1 74.1 us: on_device(): lax.all_gather(embed_table, ('wide', 'narrow'), axis=0, tiled=True)]
    all_to_all x7 -> x0, other arithmetic: 179 us -> none  [on_device(): lax.all_to_all(part.astype(bf16).reshape(devices, -1), ('wide', 'narrow')...]
    unnamed x112 -> x135, local copies, waits for them, and re-layouts: 179 us -> 17.7 us
    all_gather x6 -> x0, waiting for transfers between devices: 144 us -> none  [the longest x1 60.3 us: on_device(): lax.all_gather(mlp_out, ('wide', 'narrow'), axis=0, tiled=True)]
    all_to_all x8 -> x0, local copies, waits for them, and re-layouts: 96.5 us -> none  [on_device(): lax.all_to_all(part.astype(bf16).reshape(devices, -1), ('wide', 'narrow')...]
    reduce_sum x10 -> x0, other arithmetic: 82.7 us -> none  [the longest x9 80.3 us: on_device(): jnp.sum(lax.all_to_all(part.astype(bf16).reshape(devices, -1), ('wide', '...]
  transfers between devices with their start and end apart: 15 -> 0, of which waited for: 8 -> 0; matrix products, arithmetic and copies ran while one was open for 41% -> 0% of each run, Pallas kernels for 0% -> 0%
where the time goes in v3:
time: 411 us; the launch traced here: 404 us
  Pallas kernels  298 us (73%)
  matrix products  47 us (11%)
  local copies, waits for them, and re-layouts  38.9 us (9%)
  other arithmetic  17.7 us (4%)
    pallas_call x1, Pallas kernels, scatter_all(): pl.pallas_call(functools.partial(scatter_kernel, tuple(direct), tuple(sha...  153 us
    pallas_call x1, Pallas kernels, gather_all(): pl.pallas_call(functools.partial(gather_kernel, widths, wide, narrow), ou...  144 us
    unnamed x135, local copies, waits for them, and re-layouts  17.7 us

profile of v3, /device:TPU:8, one launch (start us, length us, event | category | flops | bytes accessed | tf_op | source)
XLA Modules:
  0.0 403.5 jit_solution(17405645631451738636)
XLA Ops:
  4.0 1.4 fusion.67
  6.3 144.4 %gather_all.1 = (bf16[32,32,4096]{2,1,0:T(8,128)(2,1)}, bf16[32,128,1024]{2,1,0:T(8,128)(2,1)}, bf16[32,32,3072]{2,1,0:T(8,128)(2,1)}, bf16[32,32,3072]{2,1,0:T(...) custom-call(bf16[1024,128]{1,0:T(8,128)(2,1)} %bitcast.262, ...), custom_call_target="tpu_custom_call" | custom-call | tf_op jit(solution)/shard_map/gather_all/pallas_call | solution.py:291
  150.8 1.4 copy.151
  152.3 2.0 fusion.14
  158.7 3.4 fusion.3
  162.1 1.2 copy-done.14
  163.6 1.5 slice_multiply_fusion
  167.8 1.3 copy-done.4
  170.0 3.8 fusion.5
  177.6 5.0 %multiply_convert_fusion = (bf16[128,4096]{1,0:T(8,128)(2,1)S(1)}, f32[128,4096]{1,0:T(8,128)S(1)}) fusion(f32[4096]{0:T(1024)S(1)} %bitcast.277, bf16[1024,4096]{1,0:T(8,128)(2,1)} %bitcast.198, f32[128,1024]{1,0:T(8,128)S(1)} %get-tuple-element.118, f32[1024]{0:T(1024)S(1)} %bitcast.270, f32[1024]{0:T(1024)S(1)} %bitcast.264, f32[128]{0:T(128)S(1)} %fusion.50, ...), kind=kOutput, calls=%fused_computation.18 | convolution fusion | flops 1077542912 | bytes 12084224 | tf_op jit(solution)/shard_map/dot_general | solution.py:794
  182.7 4.3 %fusion.72 = (bf16[4096]{0:T(1024)(128)(2,1)}, bf16[128,4096]{1,0:T(8,128)(2,1)S(1)}) fusion(f32[128,4096]{1,0:T(8,128)S(1)} %get-tuple-element.120, bf16[4096,1024]{1,0:T(8,128)(2,1)S(1)} %bitcast.204, bf16[1,128,1024]{2,1,0:T(8,128)(2,1)S(1)} %copy-done.12), kind=kOutput, calls=%fused_computation.148 | convolution fusion | flops 1081077760 | bytes 11804672 | tf_op jit(solution)/shard_map/dot_general | solution.py:806
  187.0 2.0 fusion.28
  189.6 4.3 %multiply_reduce_fusion.5 = (bf16[1024]{0:T(1024)(128)(2,1)}, f32[128]{0:T(128)}, bf16[1024]{0:T(1024)(128)(2,1)}, f32[128,1024]{1,0:T(8,128)}) fusion(f32[128,1024]{1,0:T(8,128)S(1)} %get-tuple-element.118, f32[128]{0:T(128)S(1)} %fusion.50, f32[128]{0:T(128)S(1)} %broadcast_multiply_fusion.2, f32[1024]{0:T(1024)S(1)} %bitcast.265, ...), kind=kOutput, calls=%fused_computation.77 | convolution fusion | flops 1074788224 | bytes 10495488 | tf_op jit(solution)/shard_map/dot_general | solution.py:810
  193.9 1.3 reshape.360
  195.9 2.2 fusion.64
  198.6 1.3 copy.128
  200.5 1.8 copy.127
  202.3 1.1 fusion.61
  203.4 2.5 convolution_convert_fusion.3
  209.6 5.1 %multiply_reduce_fusion.6 = (bf16[1024]{0:T(1024)(128)(2,1)S(1)}, f32[128]{0:T(128)S(1)}, bf16[1024]{0:T(1024)(128)(2,1)S(1)}, f32[128,1024]{1,0:T(8,128)S(1)}) fusion(f32[128,1024]{1,0:T(8,128)S(1)} %get-tuple-element.114, f32[128]{0:T(128)S(1)} %copy-done.51, f32[128]{0:T(128)S(1)} %copy-done.48, f32[1024]{0:T(1024)S(1)} %bitcast.279, ...), kind=kOutput, calls=%fused_computation.78 | convolution fusion | flops 808712064 | bytes 8136192 | tf_op jit(solution)/shard_map/dot_general | solution.py:852
  225.3 1.4 multiply_convert_fusion.2
  226.7 3.3 fusion.12
  230.0 3.5 fusion.18
  236.1 1.4 fusion.17.refs_5_
  237.5 153.4 %scatter_all.1 = (f32[1024,128]{1,0:T(8,128)}, f32[1024,128]{1,0:T(8,128)}, f32[768,128]{1,0:T(8,128)}, f32[768,128]{1,0:T(8,128)}, f32[256,128]{1,0:T(8,128)}, /*index=5*/f32[256,128]{1,0:T(8,128)}, f32[96,128]{1,0:T(8,128)}) custom-call(bf16[8,2,64,128]{3,2,1,0:T(8,128)(2,1)} %bitcast.252, bf16[128,4096]{1,0:T(8,128)(2,1)} %copy-done.10, ...), custom_call_target="tpu_custom_call" | custom-call | tf_op jit(solution)/shard_map/scatter_all/pallas_call | solution.py:669
  390.9 1.3 slice_bitcast_fusion.3
  392.3 1.3 slice_bitcast_fusion.2
  393.6 1.4 slice_bitcast_fusion
  395.0 1.8 copy.160
  396.8 1.6 copy.161
  398.3 1.8 copy.162
  400.1 1.6 copy.163
  (231 shorter events, 36.5 us)
Async XLA Ops:
  2.4 155.1 %copy-start.53 = (bf16[256]{0:T(256)(128)(2,1)}, bf16[256]{0:T(256)(128)(2,1)S(1)}, u32[]{:S(2)}) copy-start(bf16[256]{0:T(256)(128)(2,1)S(1)} %pad.23.clone) | copy-start | bytes 1540
  6.3 160.8 %copy-start.15 = (f32[5,48,128]{2,1,0:T(8,128)}, f32[5,48,128]{2,1,0:T(8,128)S(1)}, u32[]{:S(2)}) copy-start(f32[5,48,128]{2,1,0:T(8,128)S(1)} %concatenate.31) | copy-start | bytes 368644
  154.2 9.3 %copy-start.38 = (f32[1024]{0:T(1024)}, f32[1024]{0:T(1024)S(1)}, u32[]{:S(2)}) copy-start(f32[1024]{0:T(1024)S(1)} %convert_convert_fusion) | copy-start | bytes 12292
  154.9 15.1 %copy-start.34 = (f32[1,1024]{1,0:T(1,128)}, f32[1,1024]{1,0:T(1,128)S(1)}, u32[]{:S(2)}) copy-start(f32[1,1024]{1,0:T(1,128)S(1)} %get-tuple-element.106) | copy-start | bytes 12292
  154.9 15.1 %copy-start.36 = (f32[1,1024]{1,0:T(1,128)}, f32[1,1024]{1,0:T(1,128)S(1)}, u32[]{:S(2)}) copy-start(f32[1,1024]{1,0:T(1,128)S(1)} %get-tuple-element.107) | copy-start | bytes 12292
  163.6 3.8 copy-start.7
  167.3 2.4 copy-start.2
  167.8 2.2 copy-start.23
  169.8 4.1 %copy-start.47 = (f32[128]{0:T(128)}, f32[128]{0:T(128)S(1)}, u32[]{:S(2)}) copy-start(f32[128]{0:T(128)S(1)} %broadcast_multiply_fusion.3) | copy-start | bytes 1540
  170.0 3.9 copy-start.55
  170.0 3.9 copy-start.50
  176.2 6.4 %slice-start.2 = ((s8[8388608]{0:T(1024)(128)(4,1)}), s8[4194304]{0:T(1024)(128)(4,1)S(1)}, s32[]{:S(2)}) async-start(s8[8388608]{0:T(1024)(128)(4,1)} %bitcast.202), calls=%async_computation.2 | async-start | bytes 8388608
  176.8 12.1 %copy-start.44 = (f32[128]{0:T(128)}, f32[128]{0:T(128)S(1)}, u32[]{:S(2)}) copy-start(f32[128]{0:T(128)S(1)} %broadcast_multiply_fusion.2) | copy-start | bytes 1540
  177.5 11.4 %copy-start.45 = (f32[128]{0:T(128)}, f32[128]{0:T(128)S(1)}, u32[]{:S(2)}) copy-start(f32[128]{0:T(128)S(1)} %fusion.50) | copy-start | bytes 1540
  177.6 5.1 %slice-start.3 = ((s8[8388608]{0:T(1024)(128)(4,1)}), s8[4194304]{0:T(1024)(128)(4,1)S(1)}, s32[]{:S(2)}) async-start(s8[8388608]{0:T(1024)(128)(4,1)} %bitcast.202), calls=%async_computation.3 | async-start | bytes 8388608
  177.6 5.1 %copy-start.12 = (bf16[1,128,1024]{2,1,0:T(8,128)(2,1)S(1)}, bf16[1,128,1024]{2,1,0:T(8,128)(2,1)}, u32[]{:S(2)}) copy-start(bf16[1,128,1024]{2,1,0:T(8,128)(2,1)} %param.25) | copy-start | bytes 786436
  182.6 4.3 %copy-start.41 = (f32[1,1024]{1,0:T(1,128)S(1)}, f32[1,1024]{1,0:T(1,128)}, u32[]{:S(2)}) copy-start(f32[1,1024]{1,0:T(1,128)} %get-tuple-element.102) | copy-start | bytes 12292
  182.7 6.3 %slice-start = ((s8[8388608]{0:T(1024)(128)(4,1)}), s8[4194304]{0:T(1024)(128)(4,1)S(1)}, s32[]{:S(2)}) async-start(s8[8388608]{0:T(1024)(128)(4,1)} %bitcast.199), calls=%async_computation | async-start | bytes 8388608
  186.9 2.7 slice-start.1
  198.0 4.3 %copy-start.9 = (f32[128,1024]{1,0:T(8,128)S(1)}, f32[128,1024]{1,0:T(8,128)}, u32[]{:S(2)}) copy-start(f32[128,1024]{1,0:T(8,128)} %get-tuple-element.94) | copy-start | bytes 1572868
  203.4 2.6 copy-start.25
  203.4 4.0 copy-start.18
  209.6 6.1 %copy-start.56 = (f32[128]{0:T(128)S(1)}, f32[128]{0:T(128)}, u32[]{:S(2)}) copy-start(f32[128]{0:T(128)} %copy-done.55) | copy-start | bytes 1540
  209.6 6.1 %copy-start.37 = (f32[1,1024]{1,0:T(1,128)S(1)}, f32[1,1024]{1,0:T(1,128)}, u32[]{:S(2)}) copy-start(f32[1,1024]{1,0:T(1,128)} %copy-done.36) | copy-start | bytes 12292
  218.3 2.9 copy-start.8
  219.4 2.3 copy-start.16
  230.0 3.6 copy-start.40
  230.0 3.7 copy-start.42
  230.0 3.7 copy-start.43
  390.9 10.7 %copy-start.30 = (f32[1024,128]{1,0:T(8,128)S(1)}, f32[1024,128]{1,0:T(8,128)}, u32[]{:S(2)}) copy-start(f32[1024,128]{1,0:T(8,128)} %get-tuple-element.37) | copy-start | bytes 1572868
  390.9 11.6 %copy-start.29 = (f32[1024,128]{1,0:T(8,128)S(1)}, f32[1024,128]{1,0:T(8,128)}, u32[]{:S(2)}) copy-start(f32[1024,128]{1,0:T(8,128)} %get-tuple-element.38) | copy-start | bytes 1572868
  393.6 9.7 %copy-start.1 = (bf16[1,48,4,128]{3,2,1,0:T(4,128)(2,1)S(1)}, bf16[1,48,4,128]{3,2,1,0:T(4,128)(2,1)}, u32[]{:S(2)}) copy-start(bf16[1,48,4,128]{3,2,1,0:T(4,128)(2,1)} %param.13) | copy-start | bytes 147460
  (30 other events, 44.9 us)
